TPU v7x, 256 devices: a whole 4x4x8 slice. The times are simulated.
256 devices in a mesh: tx: 8 (over x, core), gz: 32 (over y, z).
Axes of the slice: x: 4, y: 4, z: 8, core: 2. Of those that a mesh axis runs over, the one named last changes fastest.
Arguments:
- sources: float32 [8, 2, 128, 128, 128], P('tx', None, 'gz'), may hold values from -2 to 2
- contrast: float32 [2, 128, 128, 128], P(None, 'gz'), may hold values from -3 to 3
- spectrum: float32 [2, 256, 256, 256], P(None, None, 'gz'), may hold values from -6 to 6
- measured: float32 [8, 2, 1024], P('tx'), may hold values from -6.1 to 6.1
- receivers: int32 [8, 1024], P('tx'), may hold values from 0 to 2097151
- positions: int32 [8, 2], P('tx'), may hold values from 0 to 127
Outputs:
- sources_new: float32 [8, 2, 128, 128, 128], P('tx', None, 'gz')
- contrast_new: float32 [2, 128, 128, 128], P(None, 'gz')
All inputs are finite; a program needn't handle non-finite values.
Results may differ from a plain program's by a relative error of at most 0.0001.
Values sent between devices are 32-bit elements; how exact they have to be, the bound alone decides.
A program may use at most 256 MiB of HBM per device.

v0:
```python
import math

import jax
import jax.numpy as jnp
from jax import lax
from jax.sharding import PartitionSpec as P

wave_number = 2.0 * math.pi / 12.0
reach_cells = 16.0
tikhonov = 1.0
step_length = 0.5
norm_floor = 1e-06


def dft_tables(count_out, count_in, conj_sign, divisor, period):
    out_index = lax.broadcasted_iota(jnp.int32, (count_out, count_in), 0)
    in_index = lax.broadcasted_iota(jnp.int32, (count_out, count_in), 1)
    angles = (out_index * in_index % period).astype(jnp.float32) * (2.0 * math.pi / period)
    cosine = jnp.cos(angles) / divisor
    sine_part = conj_sign * jnp.sin(angles) / divisor
    return (cosine, sine_part - cosine, cosine + sine_part)


def transform_dim(tables, real_part, imag_part, pattern):
    cos_table, minus_table, plus_table = tables
    highest = lax.Precision.HIGHEST
    prod_sum = jnp.einsum(
        pattern,
        cos_table,
        real_part + imag_part,
        precision=highest,
        preferred_element_type=jnp.float32,
    )
    prod_real = jnp.einsum(
        pattern, minus_table, real_part, precision=highest, preferred_element_type=jnp.float32
    )
    prod_imag = jnp.einsum(
        pattern, plus_table, imag_part, precision=highest, preferred_element_type=jnp.float32
    )
    return (prod_sum - prod_imag, prod_sum + prod_real)


def convolve(real_part, imag_part, spectrum, conj_sign):
    domain_width = real_part.shape[2]
    padded_width = 2 * domain_width
    forward_tables = dft_tables(padded_width, domain_width, -1.0, 1.0, padded_width)
    inverse_tables = dft_tables(domain_width, padded_width, 1.0, float(padded_width), padded_width)
    spec_real = spectrum[0][None]
    spec_imag = conj_sign * spectrum[1][None]
    real_out, imag_out = transform_dim(forward_tables, real_part, imag_part, "kq,bpqr->bpkr")
    received = lax.all_to_all(
        jnp.stack([real_out, imag_out], 1), "gz", split_axis=3, concat_axis=2, tiled=True
    )
    real_mid, imag_mid = transform_dim(
        forward_tables, received[:, 0], received[:, 1], "kp,bpqr->bkqr"
    )
    real_mid, imag_mid = transform_dim(forward_tables, real_mid, imag_mid, "kr,bpqr->bpqk")
    real_mid, imag_mid = (
        real_mid * spec_real - imag_mid * spec_imag,
        real_mid * spec_imag + imag_mid * spec_real,
    )
    real_mid, imag_mid = transform_dim(inverse_tables, real_mid, imag_mid, "kr,bpqr->bpqk")
    real_mid, imag_mid = transform_dim(inverse_tables, real_mid, imag_mid, "kp,bpqr->bkqr")
    merged = lax.all_to_all(
        jnp.stack([real_mid, imag_mid], 1), "gz", split_axis=2, concat_axis=3, tiled=True
    )
    real_out, imag_out = transform_dim(inverse_tables, merged[:, 0], merged[:, 1], "kq,bpqr->bpkr")
    return (real_out, imag_out)


def place_one(cell_index, values, slab_cells):
    return jnp.zeros((2, slab_cells), jnp.float32).at[:, cell_index].add(values)


def shards(sources, contrast, spectrum, measured, receivers, positions):
    tx_count = sources.shape[0]
    slab_planes = sources.shape[2]
    domain_width = sources.shape[3]
    plane_cells = domain_width * domain_width
    slab_cells = slab_planes * plane_cells
    data_norm = lax.psum(jnp.sum(measured * measured), "tx")
    offset = lax.axis_index("gz") * slab_planes
    grid_shape = (slab_planes, domain_width, domain_width)
    first_axis = lax.broadcasted_iota(jnp.int32, grid_shape, 0) + offset + domain_width // 4
    along_second = (
        lax.broadcasted_iota(jnp.int32, grid_shape, 1)[None] - positions[:, 0][:, None, None, None]
    )
    along_third = (
        lax.broadcasted_iota(jnp.int32, grid_shape, 2)[None] - positions[:, 1][:, None, None, None]
    )
    squared = (
        first_axis[None] * first_axis[None]
        + along_second * along_second
        + along_third * along_third
    )
    radius = jnp.sqrt(squared.astype(jnp.float32))
    amplitude = reach_cells / (reach_cells + radius)
    inc_real = amplitude * jnp.cos(wave_number * radius)
    inc_imag = amplitude * jnp.sin(wave_number * radius)
    src_real = sources[:, 0]
    src_imag = sources[:, 1]
    scat_real, scat_imag = convolve(src_real, src_imag, spectrum, 1.0)
    total_real = inc_real + scat_real
    total_imag = inc_imag + scat_imag
    numer_real = jnp.sum(src_real * total_real + src_imag * total_imag, 0)
    numer_imag = jnp.sum(src_imag * total_real - src_real * total_imag, 0)
    weight = jnp.sum(total_real * total_real + total_imag * total_imag, 0)
    numer_real, numer_imag, weight = lax.psum((numer_real, numer_imag, weight), "tx")
    chi_real = (numer_real + tikhonov * contrast[0]) / (weight + tikhonov)
    chi_imag = (numer_imag + tikhonov * contrast[1]) / (weight + tikhonov)
    contrast_new = jnp.stack([chi_real, chi_imag])
    inc_power = inc_real * inc_real + inc_imag * inc_imag
    chi_power = chi_real * chi_real + chi_imag * chi_imag
    object_local = jnp.sum(chi_power[None] * inc_power)
    local_index = receivers - offset * plane_cells
    inside = (local_index >= 0) & (local_index < slab_cells)
    clipped = jnp.clip(local_index, 0, slab_cells - 1)
    object_norm = lax.psum(object_local, ("tx", "gz"))
    norm_ratio = object_norm / (data_norm + norm_floor)
    res_real = chi_real[None] * total_real - chi_imag[None] * total_imag - src_real
    res_imag = chi_real[None] * total_imag + chi_imag[None] * total_real - src_imag
    flat_scat = jnp.stack([scat_real, scat_imag], 1).reshape(tx_count, 2, slab_cells)
    gather_index = jnp.broadcast_to(clipped[:, None, :], measured.shape)
    sampled = jnp.take_along_axis(flat_scat, gather_index, 2)
    misfit = jnp.where(inside[:, None, :], measured - sampled, 0.0)
    placed = jax.vmap(partial_place(slab_cells))(clipped, misfit)
    placed = placed.reshape(tx_count, 2, slab_planes, domain_width, domain_width)
    drive_real = norm_ratio * placed[:, 0] - (chi_real[None] * res_real + chi_imag[None] * res_imag)
    drive_imag = norm_ratio * placed[:, 1] - (chi_real[None] * res_imag - chi_imag[None] * res_real)
    back_real, back_imag = convolve(drive_real, drive_imag, spectrum, -1.0)
    new_real = src_real + step_length * (res_real + back_real)
    new_imag = src_imag + step_length * (res_imag + back_imag)
    return (jnp.stack([new_real, new_imag], 1), contrast_new)


def partial_place(slab_cells):

    def placer(cell_index, values):
        return place_one(cell_index, values, slab_cells)

    return placer


def solution(mesh):
    in_specs = (
        P("tx", None, "gz", None, None),
        P(None, "gz", None, None),
        P(None, None, "gz", None),
        P("tx", None, None),
        P("tx", None),
        P("tx", None),
    )
    out_specs = (P("tx", None, "gz", None, None), P(None, "gz", None, None))
    return jax.shard_map(shards, mesh=mesh, in_specs=in_specs, out_specs=out_specs, check_vma=False)
```

profile of v0, /device:TPU:1, one launch (start us, length us, event | category | flops | bytes accessed | tf_op | source)
XLA Modules:
  0.0 485.6 jit_solution(6261009153700445583)
XLA Ops:
  7.2 2.2 fusion.95
  9.3 2.1 fusion.39
  11.4 1.1 fusion.37
  12.7 1.3 copy.89
  14.0 12.2 %all-to-all-start = ((f32[1,2,4,256,128]{4,2,1,0,3:T(4,128)}), f32[1,2,4,256,128]{4,2,1,0,3:T(4,128)S(1)}, u32[]{:S(2)}, u32[]{:S(2)}) async-start(f32[1,2,4,256,128]{4,2,1,0,3:T(4,128)} %copy.89), calls=%async_computation | async-start | bytes 2097152 | tf_op jit(solution)/shard_map/all_to_all | solution.py:51
  26.2 3.8 fusion.377
  30.0 20.9 %all-to-all-done = f32[1,2,4,256,128]{4,2,1,0,3:T(4,128)S(1)} async-done(((f32[1,2,4,256,128]{4,2,1,0,3:T(4,128)}), f32[1,2,4,256,128]{4,2,1,0,3:T(4,128)S(1)}, u32[]{:S(2)}, u32[]{:S(2)}) %all-to-all-start) | async-done | bytes 1048608 | tf_op jit(solution)/shard_map/all_to_all | solution.py:51
  52.3 1.2 copy.161
  53.6 1.5 fusion.81
  55.1 1.5 convolution_subtract_fusion.3
  56.6 1.5 convolution_add_fusion.3
  58.2 2.3 fusion.61
  60.5 2.4 convolution_subtract_fusion.1
  62.9 4.6 fusion.17
  67.5 2.3 fusion.14
  69.8 2.4 fusion.20
  72.2 2.4 fusion.23
  74.6 2.2 fusion.66
  76.8 2.4 fusion.33
  79.3 2.3 fusion.32
  81.7 1.4 copy.102
  83.0 8.3 %all-to-all-start.1 = ((f32[1,2,128,8,128]{4,3,1,0,2:T(8,128)}), f32[1,2,128,8,128]{4,3,1,0,2:T(8,128)S(1)}, u32[]{:S(2)}, u32[]{:S(2)}) async-start(f32[1,2,128,8,128]{4,3,1,0,2:T(8,128)} %copy.102), calls=%async_computation.1 | async-start | bytes 2097152 | tf_op jit(solution)/shard_map/all_to_all | solution.py:64
  92.4 24.0 %all-to-all-done.1 = f32[1,2,128,8,128]{4,3,1,0,2:T(8,128)S(1)} async-done(((f32[1,2,128,8,128]{4,3,1,0,2:T(8,128)}), f32[1,2,128,8,128]{4,3,1,0,2:T(8,128)S(1)}, u32[]{:S(2)}, u32[]{:S(2)}) %all-to-all-start.1) | async-done | bytes 1048608 | tf_op jit(solution)/shard_map/all_to_all | solution.py:64
  117.6 2.0 copy.166
  119.7 2.0 copy.165
  121.7 2.3 fusion.78
  127.3 18.1 %gather_fusion = f32[2048]{0:T(1024)S(1)} fusion(f32[2,65536]{1,0:T(2,128)S(1)} %maximum_bitcast_fusion, s32[2048]{0:T(1024)S(1)} %bitcast.506), kind=kCustom, calls=%fused_computation | custom fusion | bytes 32768 | tf_op jit(solution)/shard_map/jit(take_along_axis)/gather | solution.py:124
  147.1 20.9 %scatter_custom_fusion = f32[65536,2]{1,0:T(8,128)} fusion(s32[1024]{0:T(1024)S(1)} %broadcast_select_fusion, f32[1024,2]{1,0:T(8,128)} %copy.111, f32[]{:T(128)} %constant.76.clone.1), kind=kCustom, calls=%fused_computation.2 | custom fusion | flops 2048 | bytes 524800
  168.0 3.4 fusion.91
  171.5 46.1 %fusion.376 = (f32[1,1,4,128,128]{1,4,3,2,0:T(8,128)}, f32[1,1,4,128,128]{1,4,3,2,0:T(8,128)}) fusion(f32[1,2,4,128,128]{1,4,3,2,0:T(8,128)} %bitcast.505), kind=kLoop, calls=%fused_computation.415 | loop fusion | bytes 1048576 | tf_op jit(solution)/shard_map/slice | solution.py:129
  217.6 17.1 %psum.39 = f32[]{:T(128)} all-reduce(f32[]{:T(128)} %get-tuple-element.31), channel_id=1, replica_groups=mesh['tx'=8,'gz'=32] {'tx'}, use_global_device_ids=true, to_apply=%region_6.7 | all-reduce | flops 1 | bytes 8 | tf_op jit(solution)/shard_map/psum | solution.py:81
  234.7 20.0 %copy.168 = f32[1,1,4,128,128]{4,3,2,1,0:T(8,128)} copy(f32[1,1,4,128,128]{1,4,3,2,0:T(8,128)} %get-tuple-element.10) | data formatting | bytes 524288
  254.8 20.0 %copy.167 = f32[1,1,4,128,128]{4,3,2,1,0:T(8,128)} copy(f32[1,1,4,128,128]{1,4,3,2,0:T(8,128)} %get-tuple-element.11) | data formatting | bytes 524288
  275.5 5.1 %multiply_reduce_fusion = (f32[]{:T(128)}, f32[4,128,128]{2,1,0:T(8,128)}, f32[4,128,128]{2,1,0:T(8,128)}) fusion(s32[]{:T(128)} %bitcast.2, s32[]{:T(128)} %bitcast.1, s32[4]{0:T(128)S(1)} %add_multiply_fusion, f32[4,128,128]{2,1,0:T(8,128)} %get-tuple-element.3, f32[4,128,128]{2,1,0:T(8,128)} %get-tuple-element.4, f32[2,4,128,128]{3,2,1,0:T(8,128)} %param.7, ...), kind=kLoop, calls=%fused_computation.149 | loop fusion | flops 1638399 | bytes 1835036 | tf_op jit(solution)/shard_map/reduce_sum | solution.py:114
  280.6 72.7 %psum.38 = f32[]{:T(128)} all-reduce(f32[]{:T(128)} %get-tuple-element.5), channel_id=1, replica_groups=mesh['tx'=8,'gz'=32] {'tx','gz'}, use_global_device_ids=true, to_apply=%region_4.5 | all-reduce | flops 1 | bytes 8 | tf_op jit(solution)/shard_map/psum | solution.py:118
  353.9 3.9 bitcast_subtract_fusion
  357.8 1.1 fusion.86
  358.9 1.1 fusion.40
  360.0 1.1 fusion.41
  361.1 1.1 pad_maximum_fusion.2
  362.2 2.6 copy.116
  364.8 30.3 %all_to_all.72 = f32[1,2,4,256,128]{4,2,1,0,3:T(4,128)S(1)} all-to-all(f32[1,2,4,256,128]{4,2,1,0,3:T(4,128)} %copy.116), channel_id=1, replica_groups=mesh['tx'=8,'gz'=32] {'gz'}, dimensions={3} | all-to-all | bytes 2097152 | tf_op jit(solution)/shard_map/all_to_all | solution.py:51
  396.4 1.2 copy.170
  397.7 2.0 copy.169
  399.7 2.6 fusion.75
  402.3 1.5 convolution_subtract_fusion.2
  403.9 1.5 convolution_add_fusion.2
  405.4 2.3 fusion.57
  407.7 2.4 convolution_subtract_fusion
  410.1 4.4 fusion.9
  414.6 2.3 fusion.6
  416.9 2.4 fusion.26
  419.3 2.4 fusion.29
  421.7 2.2 fusion.64
  423.9 2.5 fusion.35
  426.4 2.3 fusion.34
  428.8 1.4 copy.127
  430.2 8.6 %all-to-all-start.3 = ((f32[1,2,128,8,128]{4,3,1,0,2:T(8,128)}), f32[1,2,128,8,128]{4,3,1,0,2:T(8,128)S(1)}, u32[]{:S(2)}, u32[]{:S(2)}) async-start(f32[1,2,128,8,128]{4,3,1,0,2:T(8,128)} %copy.127), calls=%async_computation.3 | async-start | bytes 2097152 | tf_op jit(solution)/shard_map/all_to_all | solution.py:64
  439.6 24.2 %all-to-all-done.3 = f32[1,2,128,8,128]{4,3,1,0,2:T(8,128)S(1)} async-done(((f32[1,2,128,8,128]{4,3,1,0,2:T(8,128)}), f32[1,2,128,8,128]{4,3,1,0,2:T(8,128)S(1)}, u32[]{:S(2)}, u32[]{:S(2)}) %all-to-all-start.3) | async-done | bytes 1048608 | tf_op jit(solution)/shard_map/all_to_all | solution.py:64
  465.0 1.3 copy.172
  466.3 2.0 copy.171
  468.4 2.2 fusion.72
  470.6 3.4 fusion.51
  474.0 3.4 fusion.47
  (70 shorter events, 13.0 us)
Async XLA Ops:
  7.2 4.3 copy-start.2
  14.0 36.9 %all-to-all-start = ((f32[1,2,4,256,128]{4,2,1,0,3:T(4,128)}), f32[1,2,4,256,128]{4,2,1,0,3:T(4,128)S(1)}, u32[]{:S(2)}, u32[]{:S(2)}) async-start(f32[1,2,4,256,128]{4,2,1,0,3:T(4,128)} %copy.89), calls=%async_computation | async-start | bytes 2097152 | tf_op jit(solution)/shard_map/all_to_all | solution.py:51
  60.5 2.4 copy-start
  81.6 9.8 %copy-start.11 = (s32[1,1024]{1,0:T(1,128)S(1)}, s32[1,1024]{1,0:T(1,128)}, u32[]{:S(2)}) copy-start(s32[1,1024]{1,0:T(1,128)} %param.10) | copy-start | bytes 12292
  81.6 9.9 %copy-start.13 = (s32[1,2]{1,0:T(1,128)S(1)}, s32[1,2]{1,0:T(1,128)}, u32[]{:S(2)}) copy-start(s32[1,2]{1,0:T(1,128)} %param.11) | copy-start | bytes 28
  81.6 10.6 %copy-start.15 = (s32[2]{0:T(128)S(1)}, s32[2]{0:T(128)}, u32[]{:S(2)}) copy-start(s32[2]{0:T(128)} %constant.91) | copy-start | bytes 28
  81.6 10.7 %copy-start.14 = (s32[2]{0:T(128)S(1)}, s32[2]{0:T(128)}, u32[]{:S(2)}) copy-start(s32[2]{0:T(128)} %constant.88) | copy-start | bytes 28
  83.0 33.4 %all-to-all-start.1 = ((f32[1,2,128,8,128]{4,3,1,0,2:T(8,128)}), f32[1,2,128,8,128]{4,3,1,0,2:T(8,128)S(1)}, u32[]{:S(2)}, u32[]{:S(2)}) async-start(f32[1,2,128,8,128]{4,3,1,0,2:T(8,128)} %copy.102), calls=%async_computation.1 | async-start | bytes 2097152 | tf_op jit(solution)/shard_map/all_to_all | solution.py:64
  91.4 184.1 %all-reduce.3.cloned.1.call-start = ((), (), s32[]{:S(2)}) async-start(), calls=%async_computation.4 | async-start | bytes 1572864 | tf_op jit(solution)/shard_map/psum | solution.py:108
  126.1 0.7 copy-start.5
  127.3 18.1 %copy-start.12 = (f32[1,2,1024]{2,1,0:T(2,128)S(1)}, f32[1,2,1024]{2,1,0:T(2,128)}, u32[]{:S(2)}) copy-start(f32[1,2,1024]{2,1,0:T(2,128)} %param.9) | copy-start | bytes 24580
  147.1 20.9 %copy-start.3 = (f32[1,2,4,128,128]{4,3,2,1,0:T(8,128)S(1)}, f32[1,2,4,128,128]{4,3,2,1,0:T(8,128)}, u32[]{:S(2)}) copy-start(f32[1,2,4,128,128]{4,3,2,1,0:T(8,128)} %param.6) | copy-start | bytes 1572868
  147.1 20.9 %copy-start.6 = (f32[4,128,128]{1,2,0:T(8,128)S(1)}, f32[4,128,128]{1,2,0:T(8,128)}, u32[]{:S(2)}) copy-start(f32[4,128,128]{1,2,0:T(8,128)} %copy-done.5) | copy-start | bytes 786436
  399.7 4.1 copy-start.4
  407.7 2.4 copy-start.1
  428.8 10.0 %copy-start.8 = (f32[4,128,128]{2,1,0:T(8,128)S(1)}, f32[4,128,128]{2,1,0:T(8,128)}, u32[]{:S(2)}) copy-start(f32[4,128,128]{2,1,0:T(8,128)} %get-tuple-element.6) | copy-start | bytes 786436
  428.8 10.0 %copy-start.9 = (f32[4,128,128]{2,1,0:T(8,128)S(1)}, f32[4,128,128]{2,1,0:T(8,128)}, u32[]{:S(2)}) copy-start(f32[4,128,128]{2,1,0:T(8,128)} %get-tuple-element.7) | copy-start | bytes 786436
  430.2 33.6 %all-to-all-start.3 = ((f32[1,2,128,8,128]{4,3,1,0,2:T(8,128)}), f32[1,2,128,8,128]{4,3,1,0,2:T(8,128)S(1)}, u32[]{:S(2)}, u32[]{:S(2)}) async-start(f32[1,2,128,8,128]{4,3,1,0,2:T(8,128)} %copy.127), calls=%async_computation.3 | async-start | bytes 2097152 | tf_op jit(solution)/shard_map/all_to_all | solution.py:64
  465.0 5.5 %copy-start.7 = (f32[4,128,128]{1,2,0:T(8,128)S(1)}, f32[4,128,128]{1,2,0:T(8,128)}, u32[]{:S(2)}) copy-start(f32[4,128,128]{1,2,0:T(8,128)} %copy-done.5) | copy-start | bytes 786436
  465.0 5.5 %copy-start.10 = (f32[4,128,128]{2,1,0:T(8,128)S(1)}, f32[4,128,128]{2,1,0:T(8,128)}, u32[]{:S(2)}) copy-start(f32[4,128,128]{2,1,0:T(8,128)} %get-tuple-element.7) | copy-start | bytes 786436
Sparse Core Ops, SparseCore 0:
  171.6 64.5 all-reduce.2
where the time goes:
time: 494 us; the launch traced here: 486 us
  local copies, waits for them, and re-layouts  134 us (27%)
  blocking collectives  120 us (24%)
  matrix products  78.7 us (16%)
  waiting for transfers between devices  69.1 us (14%)
  other arithmetic  37.7 us (8%)
  starting transfers between devices  29.2 us (6%)
  between operations  16.4 us (3%)
    psum x1, blocking collectives, shards(): object_norm = lax.psum(object_local, ('tx', 'gz'))  72.7 us
    unnamed x43, local copies, waits for them, and re-layouts  53 us
    all_to_all x2, waiting for transfers between devices, convolve(): lax.all_to_all(jnp.stack([real_mid, imag_mid], 1), 'gz', split_axis=2, co...  48.2 us
    slice x1, local copies, waits for them, and re-layouts, shards(): placed[:, 1]  46.1 us
    all_to_all x1, blocking collectives, convolve(): lax.all_to_all(jnp.stack([real_out, imag_out], 1), 'gz', split_axis=3, co...  30.3 us
    dot_general x12, matrix products, transform_dim(): jnp.einsum(pattern, minus_table, real_part, precision=highest, preferred_...  29.4 us
    dot_general x12, matrix products, transform_dim(): jnp.einsum(pattern, cos_table, real_part + imag_part, precision=highest,...  25.5 us
    dot_general x12, matrix products, transform_dim(): jnp.einsum(pattern, plus_table, imag_part, precision=highest, preferred_e...  23.8 us
  transfers between devices with their start and end apart: 4, of which 3 were waited for; matrix products, arithmetic and copies ran while one was open for 19% of the time, Pallas kernels for 0%

commit v1 on v0

v1 whole, which is shorter than its diff:
```python
import math

import jax
import jax.numpy as jnp
import numpy as np
from jax import lax
from jax.experimental import pallas as pl
from jax.experimental.pallas import tpu as pltpu
from jax.sharding import PartitionSpec as P

MESH = pl.DeviceIdType.MESH
F32 = jnp.float32
BF16 = jnp.bfloat16

reach_cells = 16.0
tikhonov = 1.0
step_length = 0.5
norm_floor = 1e-06

NC = 128
NP = 256
GZ = 32
TX = 8
NREC = 1024
ROWS = 512


def dft_matrix():
    k = np.arange(NP)[:, None]
    n = np.arange(NC)[None, :]
    angle = 2.0 * np.pi * ((k * n) % NP) / NP
    cosine, sine = np.cos(angle), np.sin(angle)
    full = np.zeros((2, NP, 2, NC))
    full[0, :, 0, :] = cosine
    full[0, :, 1, :] = sine
    full[1, :, 0, :] = -sine
    full[1, :, 1, :] = cosine
    return full


def halves(table, axis):
    table = table.astype(np.float32)
    high = table.astype(jnp.bfloat16)
    low = (table - high.astype(np.float32)).astype(jnp.bfloat16)
    return np.concatenate([high, low], axis)


def dft_tables():
    full = dft_matrix()
    by_freq = full.reshape(2, GZ, 2, 4, 2, NC)
    by_plane = full.reshape(2, NP, 2, GZ, 4)
    aq = by_freq.transpose(2, 1, 0, 3, 4, 5).reshape(2 * NP, 2 * NC)
    ap = by_plane.transpose(0, 1, 2, 4, 3).reshape(2 * NP, 2 * NC)
    br = full.transpose(2, 3, 0, 1).reshape(2 * NC, 2 * NP)
    bir = full.reshape(2 * NP, 2 * NC)
    aip = by_plane.transpose(3, 2, 4, 0, 1).reshape(2 * NC, 2 * NP)
    aiq = by_freq.transpose(4, 5, 0, 2, 3, 1).reshape(2 * NC, 2 * NP)
    return (
        halves(aq, 1),
        halves(ap, 1),
        halves(br, 0),
        halves(bir, 0),
        halves(aip, 1),
        halves(aiq, 1),
    )


def split(x):
    high = x.astype(BF16)
    low = (x - high.astype(F32)).astype(BF16)
    return high, low


def left_dft(table, x):
    depth = x.shape[0]
    high, low = split(x)
    lhs = jnp.concatenate([table[:, :depth], table], axis=1)
    rhs = jnp.concatenate([high, low, high], axis=0)
    return jnp.dot(lhs, rhs, preferred_element_type=F32)


def right_dft(x, table):
    depth = x.shape[1]
    high, low = split(x)
    lhs = jnp.concatenate([high, low, high], axis=1)
    rhs = jnp.concatenate([table[:depth], table], axis=0)
    return jnp.dot(lhs, rhs, preferred_element_type=F32)


def sin_cos_twelfth(radius):
    turns = jnp.floor(radius * (1.0 / 12.0) + 0.5)
    half = (radius - 12.0 * turns) * (math.pi / 12.0)
    sq = half * half
    s = -2.5052108e-08
    for coef in (2.7557319e-06, -1.9841270e-04, 8.3333333e-03, -1.6666667e-01, 1.0):
        s = s * sq + coef
    s = s * half
    c = 2.0876757e-09
    for coef in (-2.7557319e-07, 2.4801587e-05, -1.3888889e-03, 4.1666667e-02, -0.5, 1.0):
        c = c * sq + coef
    return 2.0 * s * c, 1.0 - 2.0 * s * s


def kernel(
    src, contrast, spec_hbm, meas, cell, pos, aq, ap, br, bir, aip, aiq,
    out_src, out_chi,
    spec_raw, spec, y_buf, r_buf, u_buf, b_buf, inc, amp_sum, scat, res, drive,
    hot, part, half_in, half_sum, ring_in, chi_own, chi, extra, extra_all,
    obj, obj_all, spec_sem, send_sem, recv_sem, tx_send, tx_recv, ex_send, ex_recv,
    ob_send, ob_recv,
):
    me = lax.axis_index("gz")
    tx = lax.axis_index("tx")
    my_y = me // 8
    my_z = lax.rem(me, 8)
    my_x = tx // 2
    core = lax.rem(tx, 2)
    partner = 2 * my_x + 1 - core

    def peer_of(i):
        m = lax.rem(i, 8)
        odd = lax.rem(m, 2)
        dz = odd * ((m + 1) // 2) + (1 - odd) * (8 - m // 2)
        return lax.rem(my_y + i // 8, 4) * 8 + lax.rem(my_z + dz, 8)

    spec_copies = [
        pltpu.make_async_copy(
            spec_hbm.at[:, pl.ds(128 * n, 128)], spec_raw.at[n], spec_sem.at[n]
        )
        for n in range(2)
    ]
    for spec_copy in spec_copies:
        spec_copy.start()

    barrier = pltpu.get_barrier_semaphore()

    @pl.loop(1, GZ)
    def _(i):
        pl.semaphore_signal(barrier, inc=1, device_id={"gz": peer_of(i)}, device_id_type=MESH)

    @pl.loop(1, TX)
    def _(i):
        pl.semaphore_signal(
            barrier, inc=1, device_id={"tx": lax.rem(tx + i, TX)}, device_id_type=MESH
        )

    lane = lax.broadcasted_iota(jnp.int32, (8, 128), 1)
    share = jnp.sum(meas[...] * meas[...], keepdims=True)
    row = jnp.where(lane == 0, pos[0, 0].astype(F32), 0.0)
    row = row + jnp.where(lane == 1, pos[0, 1].astype(F32), 0.0)
    row = row + jnp.where(lane == 2, share, 0.0)
    extra[...] = row
    extra_all[pl.ds(pl.multiple_of(8 * tx, 8), 8), :] = row

    def start(sem_phase, phase, h, s_ref, d_ref):
        def block(g):
            return pl.ds(pl.multiple_of(h * 1024 + 32 * g, 32), 32)

        @pl.loop(1, GZ)
        def _(i):
            to = peer_of(i)
            pltpu.make_async_remote_copy(
                src_ref=s_ref.at[phase, block(to), :],
                dst_ref=d_ref.at[phase, block(me), :],
                send_sem=send_sem.at[sem_phase, h, to],
                recv_sem=recv_sem.at[sem_phase, h, me],
                device_id={"gz": to},
                device_id_type=MESH,
            ).start()

        d_ref[phase, block(me), :] = s_ref[phase, block(me), :]

    def wait(sem_phase, phase, h, s_ref, d_ref, receive):
        def block(g):
            return pl.ds(pl.multiple_of(h * 1024 + 32 * g, 32), 32)

        @pl.loop(1, GZ)
        def _(i):
            other = peer_of(i)
            copy = pltpu.make_async_remote_copy(
                src_ref=s_ref.at[phase, block(other), :],
                dst_ref=d_ref.at[phase, block(other), :],
                send_sem=send_sem.at[sem_phase, h, other],
                recv_sem=recv_sem.at[sem_phase, h, other],
                device_id={"gz": other},
                device_id_type=MESH,
            )
            if receive:
                copy.wait_recv()
            else:
                copy.wait_send()

    def forward_second(field, phase, ready):
        for h in range(2):
            for pp in range(2):
                x = jnp.concatenate(
                    [
                        jnp.concatenate(
                            [field[c, pl.ds((2 * pp + j) * NC, NC), :] for j in range(2)], axis=1
                        )
                        for c in range(2)
                    ],
                    axis=0,
                )
                y = left_dft(aq[pl.ds(h * 256, 256), :], x)
                for g in range(GZ):
                    for j in range(2):
                        y_buf[
                            phase, pl.ds(h * 1024 + g * 32 + (2 * pp + j) * 8, 8), :
                        ] = y[8 * g : 8 * g + 8, j * 128 : j * 128 + 128]
            if h == 0:
                ready()
            start(2 * phase, phase, h, y_buf, r_buf)

    def middle(phase, sign):
        @pl.loop(0, 2)
        def _(h):
            wait(2 * phase, phase, h, y_buf, r_buf, True)

            @pl.loop(0, 2)
            def _(jj):
                cols = []
                for j2 in range(2):
                    rows = []
                    for c in range(2):
                        for p in range(4):
                            rows.append(
                                r_buf[
                                    phase,
                                    pl.ds(h * 1024 + p * 8 + c * 4 + 2 * jj + j2, GZ, stride=32),
                                    :,
                                ]
                            )
                    cols.append(jnp.concatenate(rows, axis=0))
                z = left_dft(ap[...], jnp.concatenate(cols, axis=1))
                outs = []
                for j2 in range(2):
                    lanes = slice(j2 * NC, (j2 + 1) * NC)
                    w = right_dft(jnp.concatenate([z[:NP, lanes], z[NP:, lanes]], axis=1), br[...])
                    re, im = w[:, :NP], w[:, NP:]
                    k = h * 4 + 2 * jj + j2
                    sr, si = spec[0, k], spec[1, k] * sign
                    w = jnp.concatenate([re * sr - im * si, re * si + im * sr], axis=1)
                    v = right_dft(w, bir[...])
                    outs.append(jnp.concatenate([v[:, :NC], v[:, NC:]], axis=0))
                u = left_dft(aip[...], jnp.concatenate(outs, axis=1))
                for g in range(GZ):
                    for j2 in range(2):
                        at = pl.multiple_of(h * 1024 + g * 32 + jj * 16 + j2 * 8, 8)
                        u_buf[phase, pl.ds(at, 8), :] = u[
                            8 * g : 8 * g + 8, j2 * 128 : j2 * 128 + 128
                        ]

            start(2 * phase + 1, phase, h, u_buf, b_buf)

    def inverse_second(phase, pp):
        cols = []
        for j in range(2):
            p = 2 * pp + j
            rows = []
            for c in range(2):
                for h in range(2):
                    for k4 in range(4):
                        rows.append(
                            b_buf[
                                phase,
                                pl.ds(h * 1024 + k4 * 8 + c * 4 + p, GZ, stride=32),
                                :,
                            ]
                        )
            cols.append(jnp.concatenate(rows, axis=0))
        return left_dft(aiq[...], jnp.concatenate(cols, axis=1))

    def first_ready():
        pl.semaphore_wait(barrier, GZ - 1 + TX - 1)

    forward_second(src, 0, first_ready)

    def extra_copy(to, slot):
        return pltpu.make_async_remote_copy(
            src_ref=extra,
            dst_ref=extra_all.at[pl.ds(pl.multiple_of(8 * slot, 8), 8), :],
            send_sem=ex_send.at[to],
            recv_sem=ex_recv.at[slot],
            device_id={"tx": to},
            device_id_type=MESH,
        )

    @pl.loop(1, TX)
    def _(i):
        extra_copy(lax.rem(tx + i, TX), tx).start()

    def geometry(n, rows_n):
        index = lax.broadcasted_iota(jnp.int32, (rows_n, 128), 0) + n * rows_n
        a = lax.shift_right_logical(index, 7) + (me * 4 + NC // 4)
        b = lax.bitwise_and(index, 127)
        c = lax.broadcasted_iota(jnp.int32, (rows_n, 128), 1)
        return a, b, c

    @pl.loop(0, 16)
    def _(n):
        a, b, c = geometry(n, 32)
        b = b - pos[0, 0]
        c = c - pos[0, 1]
        radius = jnp.sqrt((a * a + b * b + c * c).astype(F32))
        amplitude = reach_cells / (reach_cells + radius)
        sine, cosine = sin_cos_twelfth(radius)
        at = pl.ds(pl.multiple_of(n * 32, 32), 32)
        inc[0, at, :] = amplitude * cosine
        inc[1, at, :] = amplitude * sine

    local = cell[...] - me * (ROWS * 128)
    cell_row = lax.shift_right_arithmetic(local, 7)
    cell_lane = lax.bitwise_and(local, 127)

    @pl.loop(0, 16)
    def _(n):
        index = lax.broadcasted_iota(jnp.int32, (32, NREC), 0) + n * 32
        hot[pl.ds(pl.multiple_of(n * 32, 32), 32), :] = jnp.where(
            index == cell_row, 1.0, 0.0
        ).astype(BF16)

    for spec_copy in spec_copies:
        spec_copy.wait()

    @pl.loop(0, 8)
    def _(k):
        for c in range(2):
            for n in range(2):
                spec[c, k, :, pl.ds(n * 128, 128)] = spec_raw[
                    n, pl.ds(c * 2048 + k, NP, stride=8), :
                ] * (2.0 ** -24)

    @pl.loop(1, TX)
    def _(i):
        other = lax.rem(tx + i, TX)
        extra_copy(other, other).wait_recv()

    @pl.loop(0, 16)
    def _(n):
        a, b, c = geometry(n, 32)
        a2 = (a * a).astype(F32)
        bf = b.astype(F32)
        cf = c.astype(F32)
        total = jnp.zeros((32, 128), F32)
        for j in range(TX):
            db = bf - extra_all[8 * j : 8 * j + 1, 0:1]
            dc = cf - extra_all[8 * j : 8 * j + 1, 1:2]
            radius = jnp.sqrt(a2 + db * db + dc * dc)
            amplitude = reach_cells / (reach_cells + radius)
            total = total + amplitude * amplitude
        amp_sum[pl.ds(pl.multiple_of(n * 32, 32), 32), :] = total

    middle(0, 1.0)

    for h in range(2):
        wait(1, 0, h, u_buf, b_buf, True)
    for pp in range(2):
        o = inverse_second(0, pp)
        for j in range(2):
            at = pl.ds((2 * pp + j) * NC, NC)
            lanes = slice(j * NC, (j + 1) * NC)
            for c in range(2):
                scat[c, at, :] = o[c * NC : (c + 1) * NC, lanes]

    @pl.loop(0, 16)
    def _(n):
        at = pl.ds(pl.multiple_of(n * 32, 32), 32)
        sr, si = src[0, at, :], src[1, at, :]
        tr = inc[0, at, :] + scat[0, at, :]
        ti = inc[1, at, :] + scat[1, at, :]
        inc[0, at, :] = tr
        inc[1, at, :] = ti
        part[0, at, :] = sr * tr + si * ti
        part[1, at, :] = si * tr - sr * ti
        part[2, at, :] = tr * tr + ti * ti

    def to_partner(s_ref, d_ref, which):
        return pltpu.make_async_remote_copy(
            src_ref=s_ref,
            dst_ref=d_ref,
            send_sem=tx_send.at[which],
            recv_sem=tx_recv.at[which],
            device_id={"tx": partner},
            device_id_type=MESH,
        )

    def half_rows(which):
        return pl.ds(pl.multiple_of(which * 256, 256), 256)

    core_copy = to_partner(part.at[:, half_rows(1 - core), :], half_in, 0)
    core_copy.start()

    pieces = []
    for c in range(2):
        pieces.append(split(scat[c]))
    columns = jnp.concatenate([pieces[0][0], pieces[1][0], pieces[0][1], pieces[1][1]], axis=1)
    found = lax.dot_general(
        columns, hot[...], (((0,), (0,)), ((), ())), preferred_element_type=F32
    )
    lane_index = lax.broadcasted_iota(jnp.int32, (NC, NREC), 0)
    on_lane = lane_index == cell_lane
    spread = []
    for c in range(2):
        both = found[c * NC : (c + 1) * NC] + found[(2 + c) * NC : (3 + c) * NC]
        sampled = jnp.sum(jnp.where(on_lane, both, 0.0), axis=0, keepdims=True)
        misfit = meas[c : c + 1, :] - sampled
        spread.append(split(jnp.where(on_lane, misfit, 0.0)))
    values = jnp.concatenate([spread[0][0], spread[1][0], spread[0][1], spread[1][1]], axis=0)
    placed = lax.dot_general(
        hot[...], values, (((1,), (1,)), ((), ())), preferred_element_type=F32
    )
    for c in range(2):
        drive[c] = placed[:, c * NC : (c + 1) * NC] + placed[:, (2 + c) * NC : (3 + c) * NC]

    core_copy.wait_recv()
    for q in range(3):
        half_sum[q] = part[q, half_rows(core), :] + half_in[q]

    def quarter(x):
        return pl.ds(pl.multiple_of(x * 64, 64), 64)

    def ring_copy(to, slot):
        return pltpu.make_async_remote_copy(
            src_ref=half_sum.at[:, quarter(to), :],
            dst_ref=ring_in.at[slot],
            send_sem=tx_send.at[1 + to],
            recv_sem=tx_recv.at[1 + slot],
            device_id={"tx": 2 * to + core},
            device_id_type=MESH,
        )

    def own_rows(x):
        return pl.ds(pl.multiple_of(core * 256 + x * 64, 64), 64)

    def chi_copy(to, slot):
        return pltpu.make_async_remote_copy(
            src_ref=chi_own,
            dst_ref=chi.at[:, own_rows(slot), :],
            send_sem=tx_send.at[5 + to],
            recv_sem=tx_recv.at[5 + slot],
            device_id={"tx": 2 * to + core},
            device_id_type=MESH,
        )

    @pl.loop(1, 4)
    def _(i):
        ring_copy(lax.rem(my_x + i, 4), my_x).start()

    ring_in[my_x] = half_sum[:, quarter(my_x), :]

    @pl.loop(1, 4)
    def _(i):
        other = lax.rem(my_x + i, 4)
        ring_copy(other, other).wait_recv()

    sums = []
    for q in range(3):
        sums.append(ring_in[0, q] + ring_in[1, q] + ring_in[2, q] + ring_in[3, q])
    below = sums[2] + tikhonov
    chi_r = (sums[0] + tikhonov * contrast[0, own_rows(my_x), :]) / below
    chi_i = (sums[1] + tikhonov * contrast[1, own_rows(my_x), :]) / below
    chi_own[0] = chi_r
    chi_own[1] = chi_i
    chi[0, own_rows(my_x), :] = chi_r
    chi[1, own_rows(my_x), :] = chi_i

    @pl.loop(1, 4)
    def _(i):
        chi_copy(lax.rem(my_x + i, 4), my_x).start()

    @pl.loop(1, 4)
    def _(i):
        other = lax.rem(my_x + i, 4)
        chi_copy(other, other).wait_recv()

    mine = chi.at[:, half_rows(core), :]
    theirs = chi.at[:, half_rows(1 - core), :]
    chi_send = to_partner(mine, mine, 9)
    chi_send.start()
    to_partner(theirs, theirs, 9).wait_recv()

    zero = jnp.zeros((32, 128), F32)

    def object_step(n, acc):
        at = pl.ds(pl.multiple_of(n * 32, 32), 32)
        cr, ci = chi[0, at, :], chi[1, at, :]
        out_chi[0, at, :] = cr
        out_chi[1, at, :] = ci
        return acc + (cr * cr + ci * ci) * amp_sum[at, :]

    acc = lax.fori_loop(0, 16, object_step, zero)
    own = acc[0:8] + acc[8:16] + acc[16:24] + acc[24:32]
    obj[...] = own
    obj_all[pl.ds(pl.multiple_of(8 * me, 8), 8), :] = own

    def obj_copy(to, slot):
        return pltpu.make_async_remote_copy(
            src_ref=obj,
            dst_ref=obj_all.at[pl.ds(pl.multiple_of(8 * slot, 8), 8), :],
            send_sem=ob_send.at[to],
            recv_sem=ob_recv.at[slot],
            device_id={"gz": to},
            device_id_type=MESH,
        )

    @pl.loop(1, GZ)
    def _(i):
        obj_copy(peer_of(i), me).start()

    @pl.loop(0, 16)
    def _(n):
        at = pl.ds(pl.multiple_of(n * 32, 32), 32)
        cr, ci = chi[0, at, :], chi[1, at, :]
        tr, ti = inc[0, at, :], inc[1, at, :]
        rr = cr * tr - ci * ti - src[0, at, :]
        ri = cr * ti + ci * tr - src[1, at, :]
        res[0, at, :] = rr
        res[1, at, :] = ri
        scat[0, at, :] = cr * rr + ci * ri
        scat[1, at, :] = cr * ri - ci * rr

    @pl.loop(1, GZ)
    def _(i):
        other = peer_of(i)
        obj_copy(other, other).wait_recv()

    object_norm = jnp.sum(obj_all[...], keepdims=True)
    data_norm = jnp.zeros((1, 1), F32)
    for j in range(TX):
        data_norm = data_norm + extra_all[8 * j : 8 * j + 1, 2:3]
    ratio = object_norm / (data_norm + norm_floor)

    @pl.loop(0, 16)
    def _(n):
        at = pl.ds(pl.multiple_of(n * 32, 32), 32)
        drive[0, at, :] = ratio * drive[0, at, :] - scat[0, at, :]
        drive[1, at, :] = ratio * drive[1, at, :] - scat[1, at, :]

    forward_second(drive, 1, lambda: None)
    middle(1, -1.0)
    for h in range(2):
        wait(3, 1, h, u_buf, b_buf, True)
    for pp in range(2):
        o = inverse_second(1, pp)
        for j in range(2):
            at = pl.ds((2 * pp + j) * NC, NC)
            lanes = slice(j * NC, (j + 1) * NC)
            for c in range(2):
                back = o[c * NC : (c + 1) * NC, lanes]
                out_src[c, at, :] = src[c, at, :] + step_length * (res[c, at, :] + back)

    for h in range(2):
        wait(0, 0, h, y_buf, r_buf, False)
        wait(1, 0, h, u_buf, b_buf, False)
        wait(2, 1, h, y_buf, r_buf, False)
        wait(3, 1, h, u_buf, b_buf, False)

    @pl.loop(1, GZ)
    def _(i):
        other = peer_of(i)
        obj_copy(other, other).wait_send()

    @pl.loop(1, TX)
    def _(i):
        other = lax.rem(tx + i, TX)
        extra_copy(other, other).wait_send()

    @pl.loop(1, 4)
    def _(i):
        other = lax.rem(my_x + i, 4)
        ring_copy(other, other).wait_send()
        chi_copy(other, other).wait_send()

    core_copy.wait_send()
    chi_send.wait_send()


def shards(sources, contrast, spectrum, measured, receivers, positions):
    vmem = pl.BlockSpec(memory_space=pltpu.VMEM)
    tables = [jnp.asarray(table) for table in dft_tables()]
    field = jax.ShapeDtypeStruct((2, ROWS, 128), F32)

    def buf(*shape):
        return pltpu.VMEM(shape, F32)

    dma = pltpu.SemaphoreType.DMA
    new, chi = pl.pallas_call(
        kernel,
        out_shape=(field, field),
        in_specs=[
            vmem,
            vmem,
            pl.BlockSpec(memory_space=pl.ANY),
            vmem,
            vmem,
            pl.BlockSpec(memory_space=pltpu.SMEM),
        ]
        + [vmem] * 6,
        out_specs=(vmem, vmem),
        scratch_shapes=[
            buf(2, 4096, 128),
            buf(2, 8, NP, NP),
            buf(2, 2048, 128),
            buf(2, 2048, 128),
            buf(2, 2048, 128),
            buf(2, 2048, 128),
            buf(2, ROWS, 128),
            buf(ROWS, 128),
            buf(2, ROWS, 128),
            buf(2, ROWS, 128),
            buf(2, ROWS, 128),
            pltpu.VMEM((ROWS, NREC), BF16),
            buf(3, ROWS, 128),
            buf(3, 256, 128),
            buf(3, 256, 128),
            buf(4, 3, 64, 128),
            buf(2, 64, 128),
            buf(2, ROWS, 128),
            buf(8, 128),
            buf(64, 128),
            buf(8, 128),
            buf(256, 128),
            dma((2,)),
            dma((4, 2, GZ)),
            dma((4, 2, GZ)),
            dma((10,)),
            dma((10,)),
            dma((TX,)),
            dma((TX,)),
            dma((GZ,)),
            dma((GZ,)),
        ],
        compiler_params=pltpu.CompilerParams(
            collective_id=0, has_side_effects=True, vmem_limit_bytes=60 * 1024 * 1024
        ),
    )(
        sources.reshape(2, ROWS, 128),
        contrast.reshape(2, ROWS, 128),
        spectrum.reshape(4096, NP),
        measured.reshape(2, NREC),
        receivers,
        positions,
        *tables,
    )
    return new.reshape(sources.shape), chi.reshape(contrast.shape)


def solution(mesh):
    in_specs = (
        P("tx", None, "gz", None, None),
        P(None, "gz", None, None),
        P(None, None, "gz", None),
        P("tx", None, None),
        P("tx", None),
        P("tx", None),
    )
    out_specs = (P("tx", None, "gz", None, None), P(None, "gz", None, None))
    return jax.shard_map(shards, mesh=mesh, in_specs=in_specs, out_specs=out_specs, check_vma=False)
```

time: 494 us -> 156 us (0.32); the launches traced: 486 us -> 156 us
  Pallas kernels: 0 us -> 151 us
  local copies, waits for them, and re-layouts: 134 us -> 3.74 us
  blocking collectives: 120 us -> 0 us
  matrix products: 78.7 us -> 0 us
  waiting for transfers between devices: 69.1 us -> 0 us
  other arithmetic: 37.7 us -> 0 us
  starting transfers between devices: 29.2 us -> 0 us
  between operations: 16.4 us -> 0.64 us
    pallas_call x0 -> x1, Pallas kernels: none -> 151 us  [shards(): pl.pallas_call(kernel, out_shape=(field, field), in_specs=[vmem, vmem, pl...]
    psum x2 -> x0, blocking collectives: 89.8 us -> none  [the longest x1 72.7 us: shards(): object_norm = lax.psum(object_local, ('tx', 'gz'))]
    dot_general x36 -> x0, matrix products: 78.7 us -> none  [the longest x12 29.4 us: transform_dim(): jnp.einsum(pattern, minus_table, real_part, precision=highest, preferred_...]
    all_to_all x3 -> x0, waiting for transfers between devices: 69.1 us -> none  [the longest x2 48.2 us: convolve(): lax.all_to_all(jnp.stack([real_mid, imag_mid], 1), 'gz', split_axis=2, co...]
    slice x7 -> x0, local copies, waits for them, and re-layouts: 54.6 us -> none  [the longest x1 46.1 us: shards(): placed[:, 1]]
    unnamed x43 -> x2, local copies, waits for them, and re-layouts: 53 us -> 3.74 us
    all_to_all x1 -> x0, blocking collectives: 30.3 us -> none  [convolve(): lax.all_to_all(jnp.stack([real_out, imag_out], 1), 'gz', split_axis=3, co...]
    all_to_all x3 -> x0, starting transfers between devices: 29.1 us -> none  [the longest x2 16.9 us: convolve(): lax.all_to_all(jnp.stack([real_mid, imag_mid], 1), 'gz', split_axis=2, co...]
  transfers between devices with their start and end apart: 4 -> 0, of which waited for: 3 -> 0; matrix products, arithmetic and copies ran while one was open for 19% -> 0% of each run, Pallas kernels for 0% -> 0%
where the time goes in v1:
time: 156 us
  Pallas kernels  151 us (97%)
  local copies, waits for them, and re-layouts  3.74 us (2%)
    pallas_call x1, Pallas kernels, shards(): pl.pallas_call(kernel, out_shape=(field, field), in_specs=[vmem, vmem, pl...  151 us
    unnamed x2, local copies, waits for them, and re-layouts  3.74 us

profile of v1, /device:TPU:1, one launch (start us, length us, event | category | flops | bytes accessed | tf_op | source)
XLA Modules:
  0.0 155.8 jit_solution(14529301453819551270)
XLA Ops:
  0.6 151.4 %shard_map.131 = (f32[2,512,128]{2,1,0:T(8,128)}, f32[2,512,128]{2,1,0:T(8,128)}) custom-call(f32[2,512,128]{2,1,0:T(8,128)} %bitcast.7, f32[2,512,128]{2,1,0:T(8,128)} %bitcast.8, f32[4096,256]{1,0:T(8,128)} %bitcast.6, f32[2,1024]{1,0:T(2,128)} %bitcast.11, s32[1,1024]{1,0:T(1,128)} %cell.1, s32[1,2]{1,0:T(1,128)} %pos.1, ...), custom_call_target="tpu_custom_call" | custom-call | tf_op jit(solution)/shard_map/pallas_call | solution.py:588
  152.1 1.9 %copy.16 = f32[1,2,4,128,128]{4,3,2,1,0:T(8,128)} copy(f32[1,2,4,128,128]{4,3,2,1,0:T(8,128)} %bitcast.10) | data formatting | bytes 1048576
  154.0 1.9 %copy.17 = f32[2,4,128,128]{3,2,1,0:T(8,128)} copy(f32[2,4,128,128]{3,2,1,0:T(8,128)} %bitcast.9) | data formatting | bytes 1048576

commit v2 on v1

v2 whole, which is shorter than its diff:
```python
import math

import jax
import jax.numpy as jnp
import numpy as np
from jax import lax
from jax.experimental import pallas as pl
from jax.experimental.pallas import tpu as pltpu
from jax.sharding import PartitionSpec as P

MESH = pl.DeviceIdType.MESH
F32 = jnp.float32
BF16 = jnp.bfloat16

reach_cells = 16.0
tikhonov = 1.0
step_length = 0.5
norm_floor = 1e-06

NC = 128
NP = 256
GZ = 32
TX = 8
NREC = 1024
ROWS = 512


def dft_matrix():
    k = np.arange(NP)[:, None]
    n = np.arange(NC)[None, :]
    angle = 2.0 * np.pi * ((k * n) % NP) / NP
    cosine, sine = np.cos(angle), np.sin(angle)
    full = np.zeros((2, NP, 2, NC))
    full[0, :, 0, :] = cosine
    full[0, :, 1, :] = sine
    full[1, :, 0, :] = -sine
    full[1, :, 1, :] = cosine
    return full


def halves(table, axis):
    table = table.astype(np.float32)
    high = table.astype(jnp.bfloat16)
    low = (table - high.astype(np.float32)).astype(jnp.bfloat16)
    return np.concatenate([high, low], axis)


def dft_tables():
    full = dft_matrix()
    by_freq = full.reshape(2, GZ, 2, 4, 2, NC)
    by_pair = full.reshape(2, GZ, 4, 2, 2, NC)
    by_plane = full.reshape(2, NP, 2, GZ, 4)
    by_half = full.reshape(2, NP, 2, GZ, 2, 2)
    aq = by_freq.transpose(2, 1, 0, 3, 4, 5).reshape(2 * NP, 2 * NC)
    ap = by_plane.transpose(0, 1, 2, 4, 3).reshape(2 * NP, 2 * NC)
    br = full.transpose(2, 3, 0, 1).reshape(2 * NC, 2 * NP)
    bir = full.reshape(2 * NP, 2 * NC)
    aip = by_half.transpose(3, 4, 2, 5, 0, 1).reshape(2 * NC, 2 * NP)
    aiq = by_pair.transpose(4, 5, 0, 2, 3, 1).reshape(2 * NC, 2 * NP)
    return (
        halves(aq, 1),
        halves(ap, 1),
        halves(br, 0),
        halves(bir, 0),
        halves(aip, 1),
        halves(aiq, 1),
    )


def split(x):
    high = x.astype(BF16)
    low = (x - high.astype(F32)).astype(BF16)
    return high, low


def left_dft(table, x):
    depth = x.shape[0]
    high, low = split(x)
    lhs = jnp.concatenate([table[:, :depth], table], axis=1)
    rhs = jnp.concatenate([high, low, high], axis=0)
    return jnp.dot(lhs, rhs, preferred_element_type=F32)


def right_dft(x, table):
    depth = x.shape[1]
    high, low = split(x)
    lhs = jnp.concatenate([high, low, high], axis=1)
    rhs = jnp.concatenate([table[:depth], table], axis=0)
    return jnp.dot(lhs, rhs, preferred_element_type=F32)


def sin_cos_twelfth(radius):
    turns = jnp.floor(radius * (1.0 / 12.0) + 0.5)
    half = (radius - 12.0 * turns) * (math.pi / 12.0)
    sq = half * half
    s = -2.5052108e-08
    for coef in (2.7557319e-06, -1.9841270e-04, 8.3333333e-03, -1.6666667e-01, 1.0):
        s = s * sq + coef
    s = s * half
    c = 2.0876757e-09
    for coef in (-2.7557319e-07, 2.4801587e-05, -1.3888889e-03, 4.1666667e-02, -0.5, 1.0):
        c = c * sq + coef
    return 2.0 * s * c, 1.0 - 2.0 * s * s


def kernel(
    src, contrast, spec_hbm, meas, cell, pos, aq, ap, br, bir, aip, aiq,
    out_src, out_chi,
    spec_raw, spec, y_buf, r_buf, u_buf, b_buf, inc, amp_sum, scat, res, drive,
    hot, hot_plane, part, half_in, half_sum, ring_in, chi_own, chi, extra, extra_all,
    obj, obj_all, mf, mf_in, mf_own, mf_all, placed_freq,
    spec_sem, send_sem, recv_sem, tx_send, tx_recv, ex_send, ex_recv,
    ob_send, ob_recv, ma_send, ma_recv, mb_send, mb_recv,
):
    me = lax.axis_index("gz")
    tx = lax.axis_index("tx")
    my_y = me // 8
    my_z = lax.rem(me, 8)
    my_x = tx // 2
    core = lax.rem(tx, 2)
    partner = 2 * my_x + 1 - core

    def peer_of(i):
        m = lax.rem(i, 8)
        odd = lax.rem(m, 2)
        dz = odd * ((m + 1) // 2) + (1 - odd) * (8 - m // 2)
        return lax.rem(my_y + i // 8, 4) * 8 + lax.rem(my_z + dz, 8)

    spec_copies = [
        pltpu.make_async_copy(
            spec_hbm.at[:, pl.ds(128 * n, 128)], spec_raw.at[n], spec_sem.at[n]
        )
        for n in range(2)
    ]
    for spec_copy in spec_copies:
        spec_copy.start()

    barrier = pltpu.get_barrier_semaphore()

    @pl.loop(1, GZ)
    def _(i):
        pl.semaphore_signal(barrier, inc=1, device_id={"gz": peer_of(i)}, device_id_type=MESH)

    @pl.loop(1, TX)
    def _(i):
        pl.semaphore_signal(
            barrier, inc=1, device_id={"tx": lax.rem(tx + i, TX)}, device_id_type=MESH
        )

    lane = lax.broadcasted_iota(jnp.int32, (8, 128), 1)
    share = jnp.sum(meas[...] * meas[...], keepdims=True)
    row = jnp.where(lane == 0, pos[0, 0].astype(F32), 0.0)
    row = row + jnp.where(lane == 1, pos[0, 1].astype(F32), 0.0)
    row = row + jnp.where(lane == 2, share, 0.0)
    extra[...] = row
    extra_all[pl.ds(pl.multiple_of(8 * tx, 8), 8), :] = row

    def exchange_copy(sem_phase, chunk, offset, size, s_ref, d_ref, to, slot):
        phase = sem_phase // 2

        def block(g):
            return pl.ds(pl.multiple_of(offset + 32 * g, 8), size)

        return pltpu.make_async_remote_copy(
            src_ref=s_ref.at[phase, block(to), :],
            dst_ref=d_ref.at[phase, block(slot), :],
            send_sem=send_sem.at[sem_phase, chunk, to],
            recv_sem=recv_sem.at[sem_phase, chunk, slot],
            device_id={"gz": to},
            device_id_type=MESH,
        )

    def start(sem_phase, chunk, offset, size, s_ref, d_ref):
        @pl.loop(1, GZ)
        def _(i):
            exchange_copy(sem_phase, chunk, offset, size, s_ref, d_ref, peer_of(i), me).start()

        phase = sem_phase // 2
        own = pl.ds(pl.multiple_of(offset + 32 * me, 8), size)
        d_ref[phase, own, :] = s_ref[phase, own, :]

    def wait(sem_phase, chunk, offset, size, s_ref, d_ref, receive=True):
        @pl.loop(1, GZ)
        def _(i):
            other = peer_of(i)
            copy = exchange_copy(sem_phase, chunk, offset, size, s_ref, d_ref, other, other)
            if receive:
                copy.wait_recv()
            else:
                copy.wait_send()

    back_chunks = ((0, 16), (16, 8), (24, 8), (1024, 32))

    def forward_second(field, phase, h, ph):
        x = jnp.concatenate(
            [
                jnp.concatenate(
                    [field[c, pl.ds((2 * ph + j) * NC, NC), :] for j in range(2)], axis=1
                )
                for c in range(2)
            ],
            axis=0,
        )
        y = left_dft(aq[pl.ds(h * 256, 256), :], x)
        for g in range(GZ):
            for j in range(2):
                y_buf[phase, pl.ds(h * 1024 + g * 32 + (2 * ph + j) * 8, 8), :] = y[
                    8 * g : 8 * g + 8, j * 128 : j * 128 + 128
                ]

    def middle(phase, sign, ratio):
        @pl.loop(0, 4)
        def _(kk):
            h = kk // 2

            @pl.when(lax.rem(kk, 2) == 0)
            def _():
                if phase == 0:
                    wait(0, h, h * 1024, 32, y_buf, r_buf)
                else:
                    for ph in range(2):
                        wait(2, 2 * ph + h, h * 1024 + ph * 16, 16, y_buf, r_buf)

            cols = []
            for i in range(2):
                rows = []
                for c in range(2):
                    for p in range(4):
                        first = h * 1024 + p * 8 + c * 4 + 2 * lax.rem(kk, 2) + i
                        x = r_buf[phase, pl.ds(first, GZ, stride=32), :]
                        if ratio is not None:
                            x = x + ratio * placed_freq[
                                2 * kk + i, c * NC + p * GZ : c * NC + (p + 1) * GZ, :
                            ]
                        rows.append(x)
                cols.append(jnp.concatenate(rows, axis=0))
            z = left_dft(ap[...], jnp.concatenate(cols, axis=1))
            outs = []
            for i in range(2):
                lanes = slice(i * NC, (i + 1) * NC)
                w = right_dft(jnp.concatenate([z[:NP, lanes], z[NP:, lanes]], axis=1), br[...])
                re, im = w[:, :NP], w[:, NP:]
                sr, si = spec[0, 2 * kk + i], spec[1, 2 * kk + i] * sign
                w = jnp.concatenate([re * sr - im * si, re * si + im * sr], axis=1)
                v = right_dft(w, bir[...])
                outs.append(jnp.concatenate([v[:, :NC], v[:, NC:]], axis=0))
            u = left_dft(aip[...], jnp.concatenate(outs, axis=1))
            upper = lax.bitwise_and(lax.broadcasted_iota(jnp.int32, (256, NC), 0), 4) != 0
            even, odd = u[:, :NC], u[:, NC:]
            halves_of_u = (
                jnp.where(upper, pltpu.roll(odd, 4, 0), even),
                jnp.where(upper, odd, pltpu.roll(even, 252, 0)),
            )
            for ph in range(2):
                for g in range(GZ):
                    at = pl.multiple_of(ph * 1024 + g * 32 + kk * 8, 8)
                    u_buf[phase, pl.ds(at, 8), :] = halves_of_u[ph][8 * g : 8 * g + 8]

            for at_kk, chunks in ((1, (0,)), (2, (1,)), (3, (2, 3))):

                @pl.when(kk == at_kk)
                def _():
                    for chunk in chunks:
                        start(2 * phase + 1, chunk, *back_chunks[chunk], u_buf, b_buf)

    def wait_back(phase, ph):
        for chunk in ((0, 1, 2), (3,))[ph]:
            wait(2 * phase + 1, chunk, *back_chunks[chunk], u_buf, b_buf)

    def inverse_second(phase, ph):
        cols = []
        for p2 in range(2):
            rows = []
            for c in range(2):
                for kk in range(4):
                    for i in range(2):
                        first = ph * 1024 + kk * 8 + i * 4 + c * 2 + p2
                        rows.append(b_buf[phase, pl.ds(first, GZ, stride=32), :])
            cols.append(jnp.concatenate(rows, axis=0))
        return left_dft(aiq[...], jnp.concatenate(cols, axis=1))

    for h in range(2):
        for ph in range(2):
            forward_second(src, 0, h, ph)
        if h == 0:
            pl.semaphore_wait(barrier, GZ - 1 + TX - 1)
        start(0, h, h * 1024, 32, y_buf, r_buf)

    def extra_copy(to, slot):
        return pltpu.make_async_remote_copy(
            src_ref=extra,
            dst_ref=extra_all.at[pl.ds(pl.multiple_of(8 * slot, 8), 8), :],
            send_sem=ex_send.at[to],
            recv_sem=ex_recv.at[slot],
            device_id={"tx": to},
            device_id_type=MESH,
        )

    @pl.loop(1, TX)
    def _(i):
        extra_copy(lax.rem(tx + i, TX), tx).start()

    def geometry(n, rows_n):
        index = lax.broadcasted_iota(jnp.int32, (rows_n, 128), 0) + n * rows_n
        a = lax.shift_right_logical(index, 7) + (me * 4 + NC // 4)
        b = lax.bitwise_and(index, 127)
        c = lax.broadcasted_iota(jnp.int32, (rows_n, 128), 1)
        return a, b, c

    @pl.loop(0, 16)
    def _(n):
        a, b, c = geometry(n, 32)
        b = b - pos[0, 0]
        c = c - pos[0, 1]
        radius = jnp.sqrt((a * a + b * b + c * c).astype(F32))
        amplitude = reach_cells / (reach_cells + radius)
        sine, cosine = sin_cos_twelfth(radius)
        at = pl.ds(pl.multiple_of(n * 32, 32), 32)
        inc[0, at, :] = amplitude * cosine
        inc[1, at, :] = amplitude * sine

    local = cell[...] - me * (ROWS * 128)
    cell_row = lax.shift_right_arithmetic(local, 7)
    cell_lane = lax.bitwise_and(local, 127)

    @pl.loop(0, 16)
    def _(n):
        index = lax.broadcasted_iota(jnp.int32, (32, NREC), 0) + n * 32
        hot[pl.ds(pl.multiple_of(n * 32, 32), 32), :] = jnp.where(
            index == cell_row, 1.0, 0.0
        ).astype(BF16)

    row_index = lax.broadcasted_iota(jnp.int32, (NC, NREC), 0)
    plane = 4 * lax.bitwise_and(row_index, 31) + lax.shift_right_logical(row_index, 5)
    hot_plane[...] = jnp.where(
        plane == lax.shift_right_logical(cell[...], 14), 1.0, 0.0
    ).astype(BF16)

    for spec_copy in spec_copies:
        spec_copy.wait()

    @pl.loop(0, 8)
    def _(k):
        for c in range(2):
            for n in range(2):
                spec[c, k, :, pl.ds(n * 128, 128)] = spec_raw[
                    n, pl.ds(c * 2048 + k, NP, stride=8), :
                ] * (2.0 ** -24)

    @pl.loop(1, TX)
    def _(i):
        other = lax.rem(tx + i, TX)
        extra_copy(other, other).wait_recv()

    @pl.loop(0, 16)
    def _(n):
        a, b, c = geometry(n, 32)
        a2 = (a * a).astype(F32)
        bf = b.astype(F32)
        cf = c.astype(F32)
        total = jnp.zeros((32, 128), F32)
        for j in range(TX):
            db = bf - extra_all[8 * j : 8 * j + 1, 0:1]
            dc = cf - extra_all[8 * j : 8 * j + 1, 1:2]
            radius = jnp.sqrt(a2 + db * db + dc * dc)
            amplitude = reach_cells / (reach_cells + radius)
            total = total + amplitude * amplitude
        amp_sum[pl.ds(pl.multiple_of(n * 32, 32), 32), :] = total

    middle(0, 1.0, None)

    def to_partner(s_ref, d_ref, which):
        return pltpu.make_async_remote_copy(
            src_ref=s_ref,
            dst_ref=d_ref,
            send_sem=tx_send.at[which],
            recv_sem=tx_recv.at[which],
            device_id={"tx": partner},
            device_id_type=MESH,
        )

    def plane_rows(p):
        return pl.ds(pl.multiple_of(p * NC, NC), NC)

    def core_copy(ph):
        return to_partner(part.at[:, plane_rows(2 * ph + 1 - core), :], half_in.at[ph], 10 * ph)

    def ring_copy(ph, to, slot):
        return pltpu.make_async_remote_copy(
            src_ref=half_sum.at[ph, :, pl.ds(pl.multiple_of(to * 32, 32), 32), :],
            dst_ref=ring_in.at[ph, slot],
            send_sem=tx_send.at[10 * ph + 1 + to],
            recv_sem=tx_recv.at[10 * ph + 1 + slot],
            device_id={"tx": 2 * to + core},
            device_id_type=MESH,
        )

    def own_rows(ph, x):
        return pl.ds(pl.multiple_of((2 * ph + core) * NC + x * 32, 32), 32)

    def chi_copy(ph, to, slot):
        return pltpu.make_async_remote_copy(
            src_ref=chi_own.at[ph],
            dst_ref=chi.at[:, own_rows(ph, slot), :],
            send_sem=tx_send.at[10 * ph + 5 + to],
            recv_sem=tx_recv.at[10 * ph + 5 + slot],
            device_id={"tx": 2 * to + core},
            device_id_type=MESH,
        )

    def chi_send(ph, which):
        at = chi.at[:, plane_rows(2 * ph + which), :]
        return to_partner(at, at, 10 * ph + 9)

    def fields(ph):
        wait_back(0, ph)
        o = inverse_second(0, ph)
        for j in range(2):
            at = pl.ds((2 * ph + j) * NC, NC)
            for c in range(2):
                scat[c, at, :] = o[c * NC : (c + 1) * NC, j * NC : (j + 1) * NC]

        @pl.loop(0, 8)
        def _(n):
            at = pl.ds(pl.multiple_of(ph * 256 + n * 32, 32), 32)
            sr, si = src[0, at, :], src[1, at, :]
            tr = inc[0, at, :] + scat[0, at, :]
            ti = inc[1, at, :] + scat[1, at, :]
            inc[0, at, :] = tr
            inc[1, at, :] = ti
            part[0, at, :] = sr * tr + si * ti
            part[1, at, :] = si * tr - sr * ti
            part[2, at, :] = tr * tr + ti * ti

        core_copy(ph).start()

    def ring_start(ph):
        core_copy(ph).wait_recv()
        for q in range(3):
            half_sum[ph, q] = part[q, plane_rows(2 * ph + core), :] + half_in[ph, q]

        @pl.loop(1, 4)
        def _(i):
            ring_copy(ph, lax.rem(my_x + i, 4), my_x).start()

        ring_in[ph, my_x] = half_sum[ph, :, pl.ds(pl.multiple_of(my_x * 32, 32), 32), :]

    def contrast_start(ph):
        @pl.loop(1, 4)
        def _(i):
            other = lax.rem(my_x + i, 4)
            ring_copy(ph, other, other).wait_recv()

        sums = []
        for q in range(3):
            sums.append(
                ring_in[ph, 0, q] + ring_in[ph, 1, q] + ring_in[ph, 2, q] + ring_in[ph, 3, q]
            )
        below = sums[2] + tikhonov
        rows = own_rows(ph, my_x)
        for c in range(2):
            value = (sums[c] + tikhonov * contrast[c, rows, :]) / below
            chi_own[ph, c] = value
            chi[c, rows, :] = value

        @pl.loop(1, 4)
        def _(i):
            chi_copy(ph, lax.rem(my_x + i, 4), my_x).start()

    def contrast_forward(ph):
        @pl.loop(1, 4)
        def _(i):
            other = lax.rem(my_x + i, 4)
            chi_copy(ph, other, other).wait_recv()

        chi_send(ph, core).start()

    def residual(ph, acc):
        chi_send(ph, 1 - core).wait_recv()

        def step(n, acc):
            at = pl.ds(pl.multiple_of(ph * 256 + n * 32, 32), 32)
            cr, ci = chi[0, at, :], chi[1, at, :]
            out_chi[0, at, :] = cr
            out_chi[1, at, :] = ci
            tr, ti = inc[0, at, :], inc[1, at, :]
            rr = cr * tr - ci * ti - src[0, at, :]
            ri = cr * ti + ci * tr - src[1, at, :]
            res[0, at, :] = rr
            res[1, at, :] = ri
            drive[0, at, :] = -(cr * rr + ci * ri)
            drive[1, at, :] = -(cr * ri - ci * rr)
            return acc + (cr * cr + ci * ci) * amp_sum[at, :]

        return lax.fori_loop(0, 8, step, acc)

    def drive_start(ph):
        for h in range(2):
            forward_second(drive, 1, h, ph)
            start(2, 2 * ph + h, h * 1024 + ph * 16, 16, y_buf, r_buf)

    def misfit_copy(to, slot):
        return pltpu.make_async_remote_copy(
            src_ref=mf.at[to // 4],
            dst_ref=mf_in.at[slot],
            send_sem=ma_send.at[to],
            recv_sem=ma_recv.at[slot],
            device_id={"gz": to},
            device_id_type=MESH,
        )

    def misfit_back(to, slot):
        return pltpu.make_async_remote_copy(
            src_ref=mf_own,
            dst_ref=mf_all.at[slot // 4],
            send_sem=mb_send.at[to // 4],
            recv_sem=mb_recv.at[slot // 4],
            device_id={"gz": to},
            device_id_type=MESH,
        )

    def group_peer(i):
        return lax.rem(me + 4 * i, GZ)

    lane_index = lax.broadcasted_iota(jnp.int32, (NC, NREC), 0)

    def misfit_start():
        pieces = [split(scat[c]) for c in range(2)]
        columns = jnp.concatenate(
            [pieces[0][0], pieces[1][0], pieces[0][1], pieces[1][1]], axis=1
        )
        found = lax.dot_general(
            columns, hot[...], (((0,), (0,)), ((), ())), preferred_element_type=F32
        )
        on_lane = lane_index == cell_lane
        inside = (cell_row >= 0) & (cell_row < ROWS)
        misfit = []
        for c in range(2):
            both = found[c * NC : (c + 1) * NC] + found[(2 + c) * NC : (3 + c) * NC]
            sampled = jnp.sum(jnp.where(on_lane, both, 0.0), axis=0, keepdims=True)
            misfit.append(jnp.where(inside, meas[c : c + 1, :] - sampled, 0.0))
        rest = jnp.zeros((6, 128), F32)
        for i in range(8):
            at = slice(i * 128, (i + 1) * 128)
            mf[i] = jnp.concatenate([misfit[0][:, at], misfit[1][:, at], rest], axis=0)
        mf_in[me] = mf[me // 4]

        @pl.loop(1, GZ)
        def _(i):
            misfit_copy(peer_of(i), me).start()

    def misfit_forward():
        @pl.loop(1, GZ)
        def _(i):
            other = peer_of(i)
            misfit_copy(other, other).wait_recv()

        total = mf_in[0]
        for g in range(1, GZ):
            total = total + mf_in[g]
        mf_own[...] = total
        mf_all[me // 4] = total

        @pl.loop(1, 8)
        def _(i):
            misfit_back(group_peer(i), me).start()

    def placed_spectrum():
        @pl.loop(1, 8)
        def _(i):
            other = group_peer(i)
            misfit_back(other, other).wait_recv()

        mr = jnp.concatenate([mf_all[i, 0:1, :] for i in range(8)], axis=1)
        mi = jnp.concatenate([mf_all[i, 1:2, :] for i in range(8)], axis=1)
        second = lax.bitwise_and(lax.shift_right_logical(cell[...], 7), 127)

        @pl.loop(0, 8)
        def _(k):
            turn = lax.bitwise_and((8 * me + k) * second, 255)
            sine, cosine = sin_cos_twelfth(turn.astype(F32) * (12.0 / 256.0))
            on_lane = lane_index == cell_lane
            v = (
                split(jnp.where(on_lane, mr * cosine + mi * sine, 0.0)),
                split(jnp.where(on_lane, mi * cosine - mr * sine, 0.0)),
            )
            values = jnp.concatenate([v[0][0], v[1][0], v[0][1], v[1][1]], axis=0)
            found = lax.dot_general(
                hot_plane[...], values, (((1,), (1,)), ((), ())), preferred_element_type=F32
            )
            for c in range(2):
                placed_freq[k, pl.ds(c * NC, NC), :] = (
                    found[:, c * NC : (c + 1) * NC] + found[:, (2 + c) * NC : (3 + c) * NC]
                )

    def obj_copy(to, slot):
        return pltpu.make_async_remote_copy(
            src_ref=obj,
            dst_ref=obj_all.at[pl.ds(pl.multiple_of(8 * slot, 8), 8), :],
            send_sem=ob_send.at[to],
            recv_sem=ob_recv.at[slot],
            device_id={"gz": to},
            device_id_type=MESH,
        )

    def object_start(acc):
        own = acc[0:8] + acc[8:16] + acc[16:24] + acc[24:32]
        obj[...] = own
        obj_all[pl.ds(pl.multiple_of(8 * me, 8), 8), :] = own

        @pl.loop(1, GZ)
        def _(i):
            obj_copy(peer_of(i), me).start()

    def object_ratio():
        @pl.loop(1, GZ)
        def _(i):
            other = peer_of(i)
            obj_copy(other, other).wait_recv()

        object_norm = jnp.sum(obj_all[...], keepdims=True)
        data_norm = jnp.zeros((1, 1), F32)
        for j in range(TX):
            data_norm = data_norm + extra_all[8 * j : 8 * j + 1, 2:3]
        return object_norm / (data_norm + norm_floor)

    fields(0)
    ring_start(0)
    contrast_start(0)
    contrast_forward(0)
    fields(1)
    acc = residual(0, jnp.zeros((32, 128), F32))
    drive_start(0)
    ring_start(1)
    misfit_start()
    contrast_start(1)
    misfit_forward()
    contrast_forward(1)
    acc = residual(1, acc)
    object_start(acc)
    drive_start(1)
    placed_spectrum()
    middle(1, -1.0, object_ratio())
    for ph in range(2):
        wait_back(1, ph)
        o = inverse_second(1, ph)
        for j in range(2):
            at = pl.ds((2 * ph + j) * NC, NC)
            for c in range(2):
                back = o[c * NC : (c + 1) * NC, j * NC : (j + 1) * NC]
                out_src[c, at, :] = src[c, at, :] + step_length * (res[c, at, :] + back)

    for h in range(2):
        wait(0, h, h * 1024, 32, y_buf, r_buf, False)
        for ph in range(2):
            wait(2, 2 * ph + h, h * 1024 + ph * 16, 16, y_buf, r_buf, False)
    for phase in range(2):
        for chunk in range(4):
            wait(2 * phase + 1, chunk, *back_chunks[chunk], u_buf, b_buf, False)

    @pl.loop(1, GZ)
    def _(i):
        other = peer_of(i)
        obj_copy(other, other).wait_send()
        misfit_copy(other, other).wait_send()

    @pl.loop(1, TX)
    def _(i):
        other = lax.rem(tx + i, TX)
        extra_copy(other, other).wait_send()

    @pl.loop(1, 8)
    def _(i):
        other = group_peer(i)
        misfit_back(other, other).wait_send()

    for ph in range(2):

        @pl.loop(1, 4)
        def _(i):
            other = lax.rem(my_x + i, 4)
            ring_copy(ph, other, other).wait_send()
            chi_copy(ph, other, other).wait_send()

        core_copy(ph).wait_send()
        chi_send(ph, core).wait_send()


def shards(sources, contrast, spectrum, measured, receivers, positions):
    vmem = pl.BlockSpec(memory_space=pltpu.VMEM)
    tables = [jnp.asarray(table) for table in dft_tables()]
    field = jax.ShapeDtypeStruct((2, ROWS, 128), F32)

    def buf(*shape):
        return pltpu.VMEM(shape, F32)

    dma = pltpu.SemaphoreType.DMA
    new, chi = pl.pallas_call(
        kernel,
        out_shape=(field, field),
        in_specs=[
            vmem,
            vmem,
            pl.BlockSpec(memory_space=pl.ANY),
            vmem,
            vmem,
            pl.BlockSpec(memory_space=pltpu.SMEM),
        ]
        + [vmem] * 6,
        out_specs=(vmem, vmem),
        scratch_shapes=[
            buf(2, 4096, 128),
            buf(2, 8, NP, NP),
            buf(2, 2048, 128),
            buf(2, 2048, 128),
            buf(2, 2048, 128),
            buf(2, 2048, 128),
            buf(2, ROWS, 128),
            buf(ROWS, 128),
            buf(2, ROWS, 128),
            buf(2, ROWS, 128),
            buf(2, ROWS, 128),
            pltpu.VMEM((ROWS, NREC), BF16),
            pltpu.VMEM((NC, NREC), BF16),
            buf(3, ROWS, 128),
            buf(2, 3, NC, 128),
            buf(2, 3, NC, 128),
            buf(2, 4, 3, 32, 128),
            buf(2, 2, 32, 128),
            buf(2, ROWS, 128),
            buf(8, 128),
            buf(64, 128),
            buf(8, 128),
            buf(256, 128),
            buf(8, 8, 128),
            buf(GZ, 8, 128),
            buf(8, 128),
            buf(8, 8, 128),
            buf(8, 2 * NC, 128),
            dma((2,)),
            dma((4, 4, GZ)),
            dma((4, 4, GZ)),
            dma((20,)),
            dma((20,)),
            dma((TX,)),
            dma((TX,)),
            dma((GZ,)),
            dma((GZ,)),
            dma((GZ,)),
            dma((GZ,)),
            dma((8,)),
            dma((8,)),
        ],
        compiler_params=pltpu.CompilerParams(
            collective_id=0, has_side_effects=True, vmem_limit_bytes=60 * 1024 * 1024
        ),
    )(
        sources.reshape(2, ROWS, 128),
        contrast.reshape(2, ROWS, 128),
        spectrum.reshape(4096, NP),
        measured.reshape(2, NREC),
        receivers,
        positions,
        *tables,
    )
    return new.reshape(sources.shape), chi.reshape(contrast.shape)


def solution(mesh):
    in_specs = (
        P("tx", None, "gz", None, None),
        P(None, "gz", None, None),
        P(None, None, "gz", None),
        P("tx", None, None),
        P("tx", None),
        P("tx", None),
    )
    out_specs = (P("tx", None, "gz", None, None), P(None, "gz", None, None))
    return jax.shard_map(shards, mesh=mesh, in_specs=in_specs, out_specs=out_specs, check_vma=False)
```

time: 156 us -> 163 us (1.045)
  Pallas kernels: 151 us -> 159 us
    pallas_call x1, Pallas kernels: 151 us -> 159 us  [shards(): pl.pallas_call(kernel, out_shape=(field, field), in_specs=[vmem, vmem, pl...]
where the time goes in v2:
time: 163 us
  Pallas kernels  159 us (98%)
  local copies, waits for them, and re-layouts  3.74 us (2%)
    pallas_call x1, Pallas kernels, shards(): pl.pallas_call(kernel, out_shape=(field, field), in_specs=[vmem, vmem, pl...  159 us
    unnamed x2, local copies, waits for them, and re-layouts  3.74 us

profile of v2, /device:TPU:1, one launch (start us, length us, event | category | flops | bytes accessed | tf_op | source)
XLA Modules:
  0.0 163.0 jit_solution(18378719329468987072)
XLA Ops:
  0.6 158.6 %shard_map.131 = (f32[2,512,128]{2,1,0:T(8,128)}, f32[2,512,128]{2,1,0:T(8,128)}) custom-call(f32[2,512,128]{2,1,0:T(8,128)} %bitcast.7, f32[2,512,128]{2,1,0:T(8,128)} %bitcast.8, f32[4096,256]{1,0:T(8,128)} %bitcast.6, f32[2,1024]{1,0:T(2,128)} %bitcast.11, s32[1,1024]{1,0:T(1,128)} %cell.1, s32[1,2]{1,0:T(1,128)} %pos.1, ...), custom_call_target="tpu_custom_call" | custom-call | tf_op jit(solution)/shard_map/pallas_call | solution.py:698
  159.2 1.9 %copy.16 = f32[1,2,4,128,128]{4,3,2,1,0:T(8,128)} copy(f32[1,2,4,128,128]{4,3,2,1,0:T(8,128)} %bitcast.10) | data formatting | bytes 1048576
  161.1 1.9 %copy.17 = f32[2,4,128,128]{3,2,1,0:T(8,128)} copy(f32[2,4,128,128]{3,2,1,0:T(8,128)} %bitcast.9) | data formatting | bytes 1048576

commit v3 on v2

--- a/solution.py
+++ b/solution.py
@@ -120,11 +120,12 @@
     core = lax.rem(tx, 2)
     partner = 2 * my_x + 1 - core
 
-    def peer_of(i):
-        m = lax.rem(i, 8)
-        odd = lax.rem(m, 2)
-        dz = odd * ((m + 1) // 2) + (1 - odd) * (8 - m // 2)
-        return lax.rem(my_y + i // 8, 4) * 8 + lax.rem(my_z + dz, 8)
+    y_part = [8 * lax.rem(my_y + d, 4) for d in range(4)]
+    z_part = [lax.rem(my_z + d, 8) for d in range(8)]
+    peers = [y_part[i // 8] + z_part[(3 * i) % 8] for i in range(1, GZ)]
+    tx_peers = [lax.rem(tx + d, TX) for d in range(1, TX)]
+    x_peers = [lax.rem(my_x + d, 4) for d in range(1, 4)]
+    group_peers = [lax.rem(me + 4 * d, GZ) for d in range(1, 8)]
 
     spec_copies = [
         pltpu.make_async_copy(
@@ -137,15 +138,10 @@
 
     barrier = pltpu.get_barrier_semaphore()
 
-    @pl.loop(1, GZ)
-    def _(i):
-        pl.semaphore_signal(barrier, inc=1, device_id={"gz": peer_of(i)}, device_id_type=MESH)
-
-    @pl.loop(1, TX)
-    def _(i):
-        pl.semaphore_signal(
-            barrier, inc=1, device_id={"tx": lax.rem(tx + i, TX)}, device_id_type=MESH
-        )
+    for to in peers:
+        pl.semaphore_signal(barrier, inc=1, device_id={"gz": to}, device_id_type=MESH)
+    for to in tx_peers:
+        pl.semaphore_signal(barrier, inc=1, device_id={"tx": to}, device_id_type=MESH)
 
     lane = lax.broadcasted_iota(jnp.int32, (8, 128), 1)
     share = jnp.sum(meas[...] * meas[...], keepdims=True)
@@ -164,30 +160,34 @@
         return pltpu.make_async_remote_copy(
             src_ref=s_ref.at[phase, block(to), :],
             dst_ref=d_ref.at[phase, block(slot), :],
-            send_sem=send_sem.at[sem_phase, chunk, to],
-            recv_sem=recv_sem.at[sem_phase, chunk, slot],
+            send_sem=send_sem.at[sem_phase, chunk],
+            recv_sem=recv_sem.at[sem_phase, chunk],
             device_id={"gz": to},
             device_id_type=MESH,
         )
 
     def start(sem_phase, chunk, offset, size, s_ref, d_ref):
-        @pl.loop(1, GZ)
-        def _(i):
-            exchange_copy(sem_phase, chunk, offset, size, s_ref, d_ref, peer_of(i), me).start()
-
+        for to in peers:
+            exchange_copy(sem_phase, chunk, offset, size, s_ref, d_ref, to, me).start()
         phase = sem_phase // 2
         own = pl.ds(pl.multiple_of(offset + 32 * me, 8), size)
         d_ref[phase, own, :] = s_ref[phase, own, :]
 
     def wait(sem_phase, chunk, offset, size, s_ref, d_ref, receive=True):
-        @pl.loop(1, GZ)
-        def _(i):
-            other = peer_of(i)
-            copy = exchange_copy(sem_phase, chunk, offset, size, s_ref, d_ref, other, other)
-            if receive:
-                copy.wait_recv()
-            else:
-                copy.wait_send()
+        phase = sem_phase // 2
+        rows = pl.ds(0, (GZ - 1) * size)
+        copy = pltpu.make_async_remote_copy(
+            src_ref=s_ref.at[phase, rows, :],
+            dst_ref=d_ref.at[phase, rows, :],
+            send_sem=send_sem.at[sem_phase, chunk],
+            recv_sem=recv_sem.at[sem_phase, chunk],
+            device_id={"gz": peers[0]},
+            device_id_type=MESH,
+        )
+        if receive:
+            copy.wait_recv()
+        else:
+            copy.wait_send()
 
     back_chunks = ((0, 16), (16, 8), (24, 8), (1024, 32))
 
@@ -286,19 +286,20 @@
             pl.semaphore_wait(barrier, GZ - 1 + TX - 1)
         start(0, h, h * 1024, 32, y_buf, r_buf)
 
-    def extra_copy(to, slot):
+    def extra_copy(to, src_ref, dst_ref):
         return pltpu.make_async_remote_copy(
-            src_ref=extra,
-            dst_ref=extra_all.at[pl.ds(pl.multiple_of(8 * slot, 8), 8), :],
-            send_sem=ex_send.at[to],
-            recv_sem=ex_recv.at[slot],
+            src_ref=src_ref,
+            dst_ref=dst_ref,
+            send_sem=ex_send,
+            recv_sem=ex_recv,
             device_id={"tx": to},
             device_id_type=MESH,
         )
 
-    @pl.loop(1, TX)
-    def _(i):
-        extra_copy(lax.rem(tx + i, TX), tx).start()
+    for to in tx_peers:
+        extra_copy(to, extra, extra_all.at[pl.ds(pl.multiple_of(8 * tx, 8), 8), :]).start()
+    extra_sum = extra_all.at[pl.ds(0, 8 * (TX - 1)), :]
+    extra_wait = extra_copy(tx_peers[0], extra_sum, extra_sum)
 
     def geometry(n, rows_n):
         index = lax.broadcasted_iota(jnp.int32, (rows_n, 128), 0) + n * rows_n
@@ -347,10 +348,7 @@
                     n, pl.ds(c * 2048 + k, NP, stride=8), :
                 ] * (2.0 ** -24)
 
-    @pl.loop(1, TX)
-    def _(i):
-        other = lax.rem(tx + i, TX)
-        extra_copy(other, other).wait_recv()
+    extra_wait.wait_recv()
 
     @pl.loop(0, 16)
     def _(n):
@@ -383,34 +381,42 @@
         return pl.ds(pl.multiple_of(p * NC, NC), NC)
 
     def core_copy(ph):
-        return to_partner(part.at[:, plane_rows(2 * ph + 1 - core), :], half_in.at[ph], 10 * ph)
-
-    def ring_copy(ph, to, slot):
+        return to_partner(part.at[:, plane_rows(2 * ph + 1 - core), :], half_in.at[ph], 4 * ph)
+
+    def ring_copy(ph, to, src_ref, dst_ref):
         return pltpu.make_async_remote_copy(
-            src_ref=half_sum.at[ph, :, pl.ds(pl.multiple_of(to * 32, 32), 32), :],
-            dst_ref=ring_in.at[ph, slot],
-            send_sem=tx_send.at[10 * ph + 1 + to],
-            recv_sem=tx_recv.at[10 * ph + 1 + slot],
+            src_ref=src_ref,
+            dst_ref=dst_ref,
+            send_sem=tx_send.at[4 * ph + 1],
+            recv_sem=tx_recv.at[4 * ph + 1],
             device_id={"tx": 2 * to + core},
             device_id_type=MESH,
         )
+
+    def ring_wait(ph):
+        three = ring_in.at[ph, pl.ds(0, 3)]
+        return ring_copy(ph, x_peers[0], three, three)
 
     def own_rows(ph, x):
         return pl.ds(pl.multiple_of((2 * ph + core) * NC + x * 32, 32), 32)
 
-    def chi_copy(ph, to, slot):
+    def chi_copy(ph, to, src_ref, dst_ref):
         return pltpu.make_async_remote_copy(
-            src_ref=chi_own.at[ph],
-            dst_ref=chi.at[:, own_rows(ph, slot), :],
-            send_sem=tx_send.at[10 * ph + 5 + to],
-            recv_sem=tx_recv.at[10 * ph + 5 + slot],
+            src_ref=src_ref,
+            dst_ref=dst_ref,
+            send_sem=tx_send.at[4 * ph + 2],
+            recv_sem=tx_recv.at[4 * ph + 2],
             device_id={"tx": 2 * to + core},
             device_id_type=MESH,
         )
+
+    def chi_wait(ph):
+        three = chi.at[:, pl.ds(0, 96), :]
+        return chi_copy(ph, x_peers[0], three, three)
 
     def chi_send(ph, which):
         at = chi.at[:, plane_rows(2 * ph + which), :]
-        return to_partner(at, at, 10 * ph + 9)
+        return to_partner(at, at, 4 * ph + 3)
 
     def fields(ph):
         wait_back(0, ph)
@@ -439,17 +445,18 @@
         for q in range(3):
             half_sum[ph, q] = part[q, plane_rows(2 * ph + core), :] + half_in[ph, q]
 
-        @pl.loop(1, 4)
-        def _(i):
-            ring_copy(ph, lax.rem(my_x + i, 4), my_x).start()
+        for to in x_peers:
+            ring_copy(
+                ph,
+                to,
+                half_sum.at[ph, :, pl.ds(pl.multiple_of(to * 32, 32), 32), :],
+                ring_in.at[ph, my_x],
+            ).start()
 
         ring_in[ph, my_x] = half_sum[ph, :, pl.ds(pl.multiple_of(my_x * 32, 32), 32), :]
 
     def contrast_start(ph):
-        @pl.loop(1, 4)
-        def _(i):
-            other = lax.rem(my_x + i, 4)
-            ring_copy(ph, other, other).wait_recv()
+        ring_wait(ph).wait_recv()
 
         sums = []
         for q in range(3):
@@ -463,16 +470,11 @@
             chi_own[ph, c] = value
             chi[c, rows, :] = value
 
-        @pl.loop(1, 4)
-        def _(i):
-            chi_copy(ph, lax.rem(my_x + i, 4), my_x).start()
+        for to in x_peers:
+            chi_copy(ph, to, chi_own.at[ph], chi.at[:, rows, :]).start()
 
     def contrast_forward(ph):
-        @pl.loop(1, 4)
-        def _(i):
-            other = lax.rem(my_x + i, 4)
-            chi_copy(ph, other, other).wait_recv()
-
+        chi_wait(ph).wait_recv()
         chi_send(ph, core).start()
 
     def residual(ph, acc):
@@ -499,28 +501,31 @@
             forward_second(drive, 1, h, ph)
             start(2, 2 * ph + h, h * 1024 + ph * 16, 16, y_buf, r_buf)
 
-    def misfit_copy(to, slot):
+    def misfit_copy(to, src_ref, dst_ref):
         return pltpu.make_async_remote_copy(
-            src_ref=mf.at[to // 4],
-            dst_ref=mf_in.at[slot],
-            send_sem=ma_send.at[to],
-            recv_sem=ma_recv.at[slot],
+            src_ref=src_ref,
+            dst_ref=dst_ref,
+            send_sem=ma_send,
+            recv_sem=ma_recv,
             device_id={"gz": to},
             device_id_type=MESH,
         )
 
-    def misfit_back(to, slot):
+    mf_most = mf_in.at[pl.ds(0, GZ - 1)]
+    misfit_wait = misfit_copy(peers[0], mf_most, mf_most)
+
+    def misfit_back(to, src_ref, dst_ref):
         return pltpu.make_async_remote_copy(
-            src_ref=mf_own,
-            dst_ref=mf_all.at[slot // 4],
-            send_sem=mb_send.at[to // 4],
-            recv_sem=mb_recv.at[slot // 4],
+            src_ref=src_ref,
+            dst_ref=dst_ref,
+            send_sem=mb_send,
+            recv_sem=mb_recv,
             device_id={"gz": to},
             device_id_type=MESH,
         )
 
-    def group_peer(i):
-        return lax.rem(me + 4 * i, GZ)
+    mf_seven = mf_all.at[pl.ds(0, 7)]
+    back_wait = misfit_back(group_peers[0], mf_seven, mf_seven)
 
     lane_index = lax.broadcasted_iota(jnp.int32, (NC, NREC), 0)
 
@@ -545,32 +550,22 @@
             mf[i] = jnp.concatenate([misfit[0][:, at], misfit[1][:, at], rest], axis=0)
         mf_in[me] = mf[me // 4]
 
-        @pl.loop(1, GZ)
-        def _(i):
-            misfit_copy(peer_of(i), me).start()
+        for to in peers:
+            misfit_copy(to, mf.at[to // 4], mf_in.at[me]).start()
 
     def misfit_forward():
-        @pl.loop(1, GZ)
-        def _(i):
-            other = peer_of(i)
-            misfit_copy(other, other).wait_recv()
-
+        misfit_wait.wait_recv()
         total = mf_in[0]
         for g in range(1, GZ):
             total = total + mf_in[g]
         mf_own[...] = total
         mf_all[me // 4] = total
 
-        @pl.loop(1, 8)
-        def _(i):
-            misfit_back(group_peer(i), me).start()
+        for to in group_peers:
+            misfit_back(to, mf_own, mf_all.at[me // 4]).start()
 
     def placed_spectrum():
-        @pl.loop(1, 8)
-        def _(i):
-            other = group_peer(i)
-            misfit_back(other, other).wait_recv()
-
+        back_wait.wait_recv()
         mr = jnp.concatenate([mf_all[i, 0:1, :] for i in range(8)], axis=1)
         mi = jnp.concatenate([mf_all[i, 1:2, :] for i in range(8)], axis=1)
         second = lax.bitwise_and(lax.shift_right_logical(cell[...], 7), 127)
@@ -593,31 +588,29 @@
                     found[:, c * NC : (c + 1) * NC] + found[:, (2 + c) * NC : (3 + c) * NC]
                 )
 
-    def obj_copy(to, slot):
+    def obj_copy(to, src_ref, dst_ref):
         return pltpu.make_async_remote_copy(
-            src_ref=obj,
-            dst_ref=obj_all.at[pl.ds(pl.multiple_of(8 * slot, 8), 8), :],
-            send_sem=ob_send.at[to],
-            recv_sem=ob_recv.at[slot],
+            src_ref=src_ref,
+            dst_ref=dst_ref,
+            send_sem=ob_send,
+            recv_sem=ob_recv,
             device_id={"gz": to},
             device_id_type=MESH,
         )
+
+    obj_most = obj_all.at[pl.ds(0, 8 * (GZ - 1)), :]
+    obj_wait = obj_copy(peers[0], obj_most, obj_most)
 
     def object_start(acc):
         own = acc[0:8] + acc[8:16] + acc[16:24] + acc[24:32]
         obj[...] = own
-        obj_all[pl.ds(pl.multiple_of(8 * me, 8), 8), :] = own
-
-        @pl.loop(1, GZ)
-        def _(i):
-            obj_copy(peer_of(i), me).start()
+        mine = pl.ds(pl.multiple_of(8 * me, 8), 8)
+        obj_all[mine, :] = own
+        for to in peers:
+            obj_copy(to, obj, obj_all.at[mine, :]).start()
 
     def object_ratio():
-        @pl.loop(1, GZ)
-        def _(i):
-            other = peer_of(i)
-            obj_copy(other, other).wait_recv()
-
+        obj_wait.wait_recv()
         object_norm = jnp.sum(obj_all[...], keepdims=True)
         data_norm = jnp.zeros((1, 1), F32)
         for j in range(TX):
@@ -658,30 +651,13 @@
         for chunk in range(4):
             wait(2 * phase + 1, chunk, *back_chunks[chunk], u_buf, b_buf, False)
 
-    @pl.loop(1, GZ)
-    def _(i):
-        other = peer_of(i)
-        obj_copy(other, other).wait_send()
-        misfit_copy(other, other).wait_send()
-
-    @pl.loop(1, TX)
-    def _(i):
-        other = lax.rem(tx + i, TX)
-        extra_copy(other, other).wait_send()
-
-    @pl.loop(1, 8)
-    def _(i):
-        other = group_peer(i)
-        misfit_back(other, other).wait_send()
-
+    obj_wait.wait_send()
+    misfit_wait.wait_send()
+    back_wait.wait_send()
+    extra_wait.wait_send()
     for ph in range(2):
-
-        @pl.loop(1, 4)
-        def _(i):
-            other = lax.rem(my_x + i, 4)
-            ring_copy(ph, other, other).wait_send()
-            chi_copy(ph, other, other).wait_send()
-
+        ring_wait(ph).wait_send()
+        chi_wait(ph).wait_send()
         core_copy(ph).wait_send()
         chi_send(ph, core).wait_send()
 
@@ -738,19 +714,12 @@
             buf(8, 8, 128),
             buf(8, 2 * NC, 128),
             dma((2,)),
-            dma((4, 4, GZ)),
-            dma((4, 4, GZ)),
-            dma((20,)),
-            dma((20,)),
-            dma((TX,)),
-            dma((TX,)),
-            dma((GZ,)),
-            dma((GZ,)),
-            dma((GZ,)),
-            dma((GZ,)),
+            dma((4, 4)),
+            dma((4, 4)),
             dma((8,)),
             dma((8,)),
-        ],
+        ]
+        + [dma] * 8,
         compiler_params=pltpu.CompilerParams(
             collective_id=0, has_side_effects=True, vmem_limit_bytes=60 * 1024 * 1024
         ),

time: 163 us -> 137 us (0.84)
  Pallas kernels: 159 us -> 132 us
    pallas_call x1, Pallas kernels: 159 us -> 132 us  [shards(): pl.pallas_call(kernel, out_shape=(field, field), in_specs=[vmem, vmem, pl...]
where the time goes in v3:
time: 137 us; the launch traced here: 136 us
  Pallas kernels  132 us (96%)
  local copies, waits for them, and re-layouts  3.74 us (3%)
    pallas_call x1, Pallas kernels, shards(): pl.pallas_call(kernel, out_shape=(field, field), in_specs=[vmem, vmem, pl...  132 us
    unnamed x2, local copies, waits for them, and re-layouts  3.74 us

profile of v3, /device:TPU:1, one launch (start us, length us, event | category | flops | bytes accessed | tf_op | source)
XLA Modules:
  0.0 136.4 jit_solution(6347463893602661814)
XLA Ops:
  0.6 132.0 %shard_map.131 = (f32[2,512,128]{2,1,0:T(8,128)}, f32[2,512,128]{2,1,0:T(8,128)}) custom-call(f32[2,512,128]{2,1,0:T(8,128)} %bitcast.7, f32[2,512,128]{2,1,0:T(8,128)} %bitcast.8, f32[4096,256]{1,0:T(8,128)} %bitcast.6, f32[2,1024]{1,0:T(2,128)} %bitcast.11, s32[1,1024]{1,0:T(1,128)} %cell.1, s32[1,2]{1,0:T(1,128)} %pos.1, ...), custom_call_target="tpu_custom_call" | custom-call | tf_op jit(solution)/shard_map/pallas_call | solution.py:674
  132.6 1.9 %copy.16 = f32[1,2,4,128,128]{4,3,2,1,0:T(8,128)} copy(f32[1,2,4,128,128]{4,3,2,1,0:T(8,128)} %bitcast.10) | data formatting | bytes 1048576
  134.5 1.9 %copy.17 = f32[2,4,128,128]{3,2,1,0:T(8,128)} copy(f32[2,4,128,128]{3,2,1,0:T(8,128)} %bitcast.9) | data formatting | bytes 1048576

commit v4 on v3

--- a/solution.py
+++ b/solution.py
@@ -45,26 +45,54 @@
     return np.concatenate([high, low], axis)
 
 
-def dft_tables():
-    full = dft_matrix()
-    by_freq = full.reshape(2, GZ, 2, 4, 2, NC)
-    by_pair = full.reshape(2, GZ, 4, 2, 2, NC)
-    by_plane = full.reshape(2, NP, 2, GZ, 4)
-    by_half = full.reshape(2, NP, 2, GZ, 2, 2)
-    aq = by_freq.transpose(2, 1, 0, 3, 4, 5).reshape(2 * NP, 2 * NC)
-    ap = by_plane.transpose(0, 1, 2, 4, 3).reshape(2 * NP, 2 * NC)
-    br = full.transpose(2, 3, 0, 1).reshape(2 * NC, 2 * NP)
-    bir = full.reshape(2 * NP, 2 * NC)
-    aip = by_half.transpose(3, 4, 2, 5, 0, 1).reshape(2 * NC, 2 * NP)
-    aiq = by_pair.transpose(4, 5, 0, 2, 3, 1).reshape(2 * NC, 2 * NP)
-    return (
-        halves(aq, 1),
-        halves(ap, 1),
-        halves(br, 0),
-        halves(bir, 0),
-        halves(aip, 1),
-        halves(aiq, 1),
-    )
+def first_table():
+    by_freq = dft_matrix().reshape(2, GZ, 2, 4, 2, NC)
+    return halves(by_freq.transpose(2, 1, 0, 3, 4, 5).reshape(2 * NP, 2 * NC), 1)
+
+
+def bits(x, shift, count):
+    return lax.bitwise_and(lax.shift_right_logical(x, shift), (1 << count) - 1)
+
+
+def freq_index(x):
+    return bits(x, 0, 8), bits(x, 8, 1)
+
+
+def freq_pair_index(x):
+    return 8 * bits(x, 0, 5) + 2 * bits(x, 6, 2) + bits(x, 5, 1), bits(x, 8, 1)
+
+
+def cell_index(x):
+    return bits(x, 0, 7), bits(x, 7, 1)
+
+
+def plane_index(x):
+    return 4 * bits(x, 0, 5) + bits(x, 5, 2), bits(x, 7, 1)
+
+
+def plane_half_index(x):
+    return 4 * bits(x, 3, 5) + 2 * bits(x, 2, 1) + bits(x, 0, 1), bits(x, 1, 1)
+
+
+def fill_table(ref, axis, row_of, column_of, rows_are_freq):
+    height, width = ref.shape
+    height, width = (height // 2, width) if axis == 0 else (height, width // 2)
+
+    @pl.loop(0, height // 32)
+    def _(n):
+        a, part_a = row_of(lax.broadcasted_iota(jnp.int32, (32, width), 0) + n * 32)
+        b, part_b = column_of(lax.broadcasted_iota(jnp.int32, (32, width), 1))
+        quarter = (part_a - part_b) if rows_are_freq else (part_b - part_a)
+        turn = lax.bitwise_and(a * b + 64 * quarter, 255)
+        table = sin_cos_twelfth(turn.astype(F32) * (12.0 / 256.0))[1]
+        high, low = split(table)
+        rows = pl.ds(pl.multiple_of(n * 32, 32), 32)
+        if axis == 0:
+            ref[rows, :] = high
+            ref[pl.ds(pl.multiple_of(height + n * 32, 32), 32), :] = low
+        else:
+            ref[rows, pl.ds(0, width)] = high
+            ref[rows, pl.ds(width, width)] = low
 
 
 def split(x):
@@ -104,12 +132,14 @@
 
 
 def kernel(
-    src, contrast, spec_hbm, meas, cell, pos, aq, ap, br, bir, aip, aiq,
-    out_src, out_chi,
+    src_hbm, contrast_hbm, spec_hbm, meas_hbm, cell_hbm, pos,
+    aq_hbm,
+    new_hbm, chi_hbm,
+    src, contrast, meas, cell, aq, ap, br, bir, aip, aiq, out_src,
     spec_raw, spec, y_buf, r_buf, u_buf, b_buf, inc, amp_sum, scat, res, drive,
     hot, hot_plane, part, half_in, half_sum, ring_in, chi_own, chi, extra, extra_all,
-    obj, obj_all, mf, mf_in, mf_own, mf_all, placed_freq,
-    spec_sem, send_sem, recv_sem, tx_send, tx_recv, ex_send, ex_recv,
+    obj, obj_all, mf, mf_in, mf_own, mf_all, placed_freq, found_first,
+    load_sem, store_sem, send_sem, recv_sem, tx_send, tx_recv, ex_send, ex_recv,
     ob_send, ob_recv, ma_send, ma_recv, mb_send, mb_recv,
 ):
     me = lax.axis_index("gz")
@@ -127,14 +157,23 @@
     x_peers = [lax.rem(my_x + d, 4) for d in range(1, 4)]
     group_peers = [lax.rem(me + 4 * d, GZ) for d in range(1, 8)]
 
-    spec_copies = [
-        pltpu.make_async_copy(
-            spec_hbm.at[:, pl.ds(128 * n, 128)], spec_raw.at[n], spec_sem.at[n]
-        )
-        for n in range(2)
-    ]
-    for spec_copy in spec_copies:
-        spec_copy.start()
+    loads = {}
+    for n, (name, hbm, vmem) in enumerate(
+        (
+            ("aq", aq_hbm, aq),
+            ("src", src_hbm, src),
+            ("meas", meas_hbm, meas),
+            ("cell", cell_hbm, cell),
+            ("spec0", spec_hbm.at[:, pl.ds(0, 128)], spec_raw.at[0]),
+            ("spec1", spec_hbm.at[:, pl.ds(128, 128)], spec_raw.at[1]),
+            ("contrast", contrast_hbm, contrast),
+        )
+    ):
+        loads[name] = pltpu.make_async_copy(hbm, vmem, load_sem.at[n])
+
+    def loaded(*names):
+        for name in names:
+            loads[name].wait()
 
     barrier = pltpu.get_barrier_semaphore()
 
@@ -142,6 +181,10 @@
         pl.semaphore_signal(barrier, inc=1, device_id={"gz": to}, device_id_type=MESH)
     for to in tx_peers:
         pl.semaphore_signal(barrier, inc=1, device_id={"tx": to}, device_id_type=MESH)
+
+    for load in loads.values():
+        load.start()
+    loaded("meas")
 
     lane = lax.broadcasted_iota(jnp.int32, (8, 128), 1)
     share = jnp.sum(meas[...] * meas[...], keepdims=True)
@@ -279,6 +322,7 @@
             cols.append(jnp.concatenate(rows, axis=0))
         return left_dft(aiq[...], jnp.concatenate(cols, axis=1))
 
+    loaded("aq", "src")
     for h in range(2):
         for ph in range(2):
             forward_second(src, 0, h, ph)
@@ -320,6 +364,7 @@
         inc[0, at, :] = amplitude * cosine
         inc[1, at, :] = amplitude * sine
 
+    loaded("cell")
     local = cell[...] - me * (ROWS * 128)
     cell_row = lax.shift_right_arithmetic(local, 7)
     cell_lane = lax.bitwise_and(local, 127)
@@ -337,8 +382,7 @@
         plane == lax.shift_right_logical(cell[...], 14), 1.0, 0.0
     ).astype(BF16)
 
-    for spec_copy in spec_copies:
-        spec_copy.wait()
+    loaded("spec0", "spec1")
 
     @pl.loop(0, 8)
     def _(k):
@@ -348,24 +392,33 @@
                     n, pl.ds(c * 2048 + k, NP, stride=8), :
                 ] * (2.0 ** -24)
 
-    extra_wait.wait_recv()
-
-    @pl.loop(0, 16)
-    def _(n):
-        a, b, c = geometry(n, 32)
-        a2 = (a * a).astype(F32)
-        bf = b.astype(F32)
-        cf = c.astype(F32)
-        total = jnp.zeros((32, 128), F32)
-        for j in range(TX):
-            db = bf - extra_all[8 * j : 8 * j + 1, 0:1]
-            dc = cf - extra_all[8 * j : 8 * j + 1, 1:2]
-            radius = jnp.sqrt(a2 + db * db + dc * dc)
-            amplitude = reach_cells / (reach_cells + radius)
-            total = total + amplitude * amplitude
-        amp_sum[pl.ds(pl.multiple_of(n * 32, 32), 32), :] = total
+    fill_table(ap, 1, freq_index, plane_index, True)
+    fill_table(br, 0, cell_index, freq_index, False)
+    fill_table(bir, 0, freq_index, cell_index, True)
+    fill_table(aip, 1, plane_half_index, freq_index, False)
+
+    def incident_power():
+        extra_wait.wait_recv()
+
+        @pl.loop(0, 16)
+        def _(n):
+            a, b, c = geometry(n, 32)
+            a2 = (a * a).astype(F32)
+            bf = b.astype(F32)
+            cf = c.astype(F32)
+            total = jnp.zeros((32, 128), F32)
+            for j in range(TX):
+                db = bf - extra_all[8 * j : 8 * j + 1, 0:1]
+                dc = cf - extra_all[8 * j : 8 * j + 1, 1:2]
+                radius = jnp.sqrt(a2 + db * db + dc * dc)
+                amplitude = reach_cells / (reach_cells + radius)
+                total = total + amplitude * amplitude
+            amp_sum[pl.ds(pl.multiple_of(n * 32, 32), 32), :] = total
 
     middle(0, 1.0, None)
+    loaded("contrast")
+    fill_table(aiq, 1, cell_index, freq_pair_index, False)
+    incident_power()
 
     def to_partner(s_ref, d_ref, which):
         return pltpu.make_async_remote_copy(
@@ -483,8 +536,6 @@
         def step(n, acc):
             at = pl.ds(pl.multiple_of(ph * 256 + n * 32, 32), 32)
             cr, ci = chi[0, at, :], chi[1, at, :]
-            out_chi[0, at, :] = cr
-            out_chi[1, at, :] = ci
             tr, ti = inc[0, at, :], inc[1, at, :]
             rr = cr * tr - ci * ti - src[0, at, :]
             ri = cr * ti + ci * tr - src[1, at, :]
@@ -496,10 +547,9 @@
 
         return lax.fori_loop(0, 8, step, acc)
 
-    def drive_start(ph):
-        for h in range(2):
-            forward_second(drive, 1, h, ph)
-            start(2, 2 * ph + h, h * 1024 + ph * 16, 16, y_buf, r_buf)
+    def drive_start(ph, h):
+        forward_second(drive, 1, h, ph)
+        start(2, 2 * ph + h, h * 1024 + ph * 16, 16, y_buf, r_buf)
 
     def misfit_copy(to, src_ref, dst_ref):
         return pltpu.make_async_remote_copy(
@@ -529,14 +579,18 @@
 
     lane_index = lax.broadcasted_iota(jnp.int32, (NC, NREC), 0)
 
-    def misfit_start():
-        pieces = [split(scat[c]) for c in range(2)]
+    def found_at(ph):
+        rows = pl.ds(ph * 256, 256)
+        pieces = [split(scat[c, rows, :]) for c in range(2)]
         columns = jnp.concatenate(
             [pieces[0][0], pieces[1][0], pieces[0][1], pieces[1][1]], axis=1
         )
-        found = lax.dot_general(
-            columns, hot[...], (((0,), (0,)), ((), ())), preferred_element_type=F32
-        )
+        return lax.dot_general(
+            columns, hot[rows, :], (((0,), (0,)), ((), ())), preferred_element_type=F32
+        )
+
+    def misfit_start():
+        found = found_first[...] + found_at(1)
         on_lane = lane_index == cell_lane
         inside = (cell_row >= 0) & (cell_row < ROWS)
         misfit = []
@@ -618,22 +672,28 @@
         return object_norm / (data_norm + norm_floor)
 
     fields(0)
+    found_first[...] = found_at(0)
     ring_start(0)
     contrast_start(0)
     contrast_forward(0)
     fields(1)
+    misfit_start()
     acc = residual(0, jnp.zeros((32, 128), F32))
-    drive_start(0)
+    drive_start(0, 0)
     ring_start(1)
-    misfit_start()
+    drive_start(0, 1)
     contrast_start(1)
     misfit_forward()
     contrast_forward(1)
     acc = residual(1, acc)
     object_start(acc)
-    drive_start(1)
+    drive_start(1, 0)
+    drive_start(1, 1)
     placed_spectrum()
+    chi_store = pltpu.make_async_copy(chi, chi_hbm, store_sem.at[2])
+    chi_store.start()
     middle(1, -1.0, object_ratio())
+    stores = []
     for ph in range(2):
         wait_back(1, ph)
         o = inverse_second(1, ph)
@@ -642,6 +702,11 @@
             for c in range(2):
                 back = o[c * NC : (c + 1) * NC, j * NC : (j + 1) * NC]
                 out_src[c, at, :] = src[c, at, :] + step_length * (res[c, at, :] + back)
+        at = pl.ds(ph * 256, 256)
+        stores.append(
+            pltpu.make_async_copy(out_src.at[:, at, :], new_hbm.at[:, at, :], store_sem.at[ph])
+        )
+        stores[-1].start()
 
     for h in range(2):
         wait(0, h, h * 1024, 32, y_buf, r_buf, False)
@@ -651,6 +716,9 @@
         for chunk in range(4):
             wait(2 * phase + 1, chunk, *back_chunks[chunk], u_buf, b_buf, False)
 
+    chi_store.wait()
+    for store in stores:
+        store.wait()
     obj_wait.wait_send()
     misfit_wait.wait_send()
     back_wait.wait_send()
@@ -663,8 +731,8 @@
 
 
 def shards(sources, contrast, spectrum, measured, receivers, positions):
-    vmem = pl.BlockSpec(memory_space=pltpu.VMEM)
-    tables = [jnp.asarray(table) for table in dft_tables()]
+    hbm = pl.BlockSpec(memory_space=pl.ANY)
+    table = jnp.asarray(first_table())
     field = jax.ShapeDtypeStruct((2, ROWS, 128), F32)
 
     def buf(*shape):
@@ -674,17 +742,20 @@
     new, chi = pl.pallas_call(
         kernel,
         out_shape=(field, field),
-        in_specs=[
-            vmem,
-            vmem,
-            pl.BlockSpec(memory_space=pl.ANY),
-            vmem,
-            vmem,
-            pl.BlockSpec(memory_space=pltpu.SMEM),
-        ]
-        + [vmem] * 6,
-        out_specs=(vmem, vmem),
+        in_specs=[hbm] * 5 + [pl.BlockSpec(memory_space=pltpu.SMEM), hbm],
+        out_specs=(hbm, hbm),
         scratch_shapes=[
+            buf(2, ROWS, 128),
+            buf(2, ROWS, 128),
+            buf(2, NREC),
+            pltpu.VMEM((1, NREC), jnp.int32),
+            pltpu.VMEM((512, 512), BF16),
+            pltpu.VMEM((512, 512), BF16),
+            pltpu.VMEM((512, 512), BF16),
+            pltpu.VMEM((1024, 256), BF16),
+            pltpu.VMEM((256, 1024), BF16),
+            pltpu.VMEM((256, 1024), BF16),
+            buf(2, ROWS, 128),
             buf(2, 4096, 128),
             buf(2, 8, NP, NP),
             buf(2, 2048, 128),
@@ -713,7 +784,9 @@
             buf(8, 128),
             buf(8, 8, 128),
             buf(8, 2 * NC, 128),
-            dma((2,)),
+            buf(512, NREC),
+            dma((7,)),
+            dma((3,)),
             dma((4, 4)),
             dma((4, 4)),
             dma((8,)),
@@ -730,7 +803,7 @@
         measured.reshape(2, NREC),
         receivers,
         positions,
-        *tables,
+        table,
     )
     return new.reshape(sources.shape), chi.reshape(contrast.shape)
 

time: 137 us -> 128 us (0.934)
  Pallas kernels: 132 us -> 123 us
    pallas_call x1, Pallas kernels: 132 us -> 123 us  [shards(): pl.pallas_call(kernel, out_shape=(field, field), in_specs=[hbm] * 5 + [pl...]
where the time goes in v4:
time: 128 us; the launch traced here: 127 us
  Pallas kernels  123 us (96%)
  local copies, waits for them, and re-layouts  3.74 us (3%)
    pallas_call x1, Pallas kernels, shards(): pl.pallas_call(kernel, out_shape=(field, field), in_specs=[hbm] * 5 + [pl...  123 us
    unnamed x2, local copies, waits for them, and re-layouts  3.74 us

profile of v4, /device:TPU:1, one launch (start us, length us, event | category | flops | bytes accessed | tf_op | source)
XLA Modules:
  0.0 127.4 jit_solution(15348266666778499586)
XLA Ops:
  0.6 123.0 %shard_map.86 = (f32[2,512,128]{2,1,0:T(8,128)}, f32[2,512,128]{2,1,0:T(8,128)}) custom-call(f32[2,512,128]{2,1,0:T(8,128)} %bitcast.9, f32[2,512,128]{2,1,0:T(8,128)} %bitcast.10, f32[4096,256]{1,0:T(8,128)} %bitcast.6, f32[2,1024]{1,0:T(2,128)} %bitcast.11, s32[1,1024]{1,0:T(1,128)} %cell_hbm.1, s32[1,2]{1,0:T(1,128)} %pos.1, ...), custom_call_target="tpu_custom_call" | custom-call | tf_op jit(solution)/shard_map/pallas_call | solution.py:742
  123.6 1.9 %copy.11 = f32[1,2,4,128,128]{4,3,2,1,0:T(8,128)} copy(f32[1,2,4,128,128]{4,3,2,1,0:T(8,128)} %bitcast.8) | data formatting | bytes 1048576
  125.5 1.9 %copy.12 = f32[2,4,128,128]{3,2,1,0:T(8,128)} copy(f32[2,4,128,128]{3,2,1,0:T(8,128)} %bitcast.7) | data formatting | bytes 1048576

commit v5 on v4

--- a/solution.py
+++ b/solution.py
@@ -194,45 +194,47 @@
     extra[...] = row
     extra_all[pl.ds(pl.multiple_of(8 * tx, 8), 8), :] = row
 
-    def exchange_copy(sem_phase, chunk, offset, size, s_ref, d_ref, to, slot):
-        phase = sem_phase // 2
-
-        def block(g):
-            return pl.ds(pl.multiple_of(offset + 32 * g, 8), size)
-
+    chunks = (
+        ((0, 1, 0, 32), (1, 1, 0, 32)),
+        ((0, 1, 0, 16), (0, 1, 16, 8), (0, 1, 24, 8), (1, 1, 0, 32)),
+        ((0, 2, 0, 16), (0, 1, 16, 16), (1, 1, 16, 16)),
+        ((0, 2, 0, 16), (0, 1, 16, 16), (1, 1, 16, 16)),
+    )
+    buffers = ((y_buf, r_buf), (u_buf, b_buf))
+
+    def exchange_copy(trip, chunk, src_at, dst_at, to):
+        phase = trip // 2
+        s_ref, d_ref = buffers[trip % 2]
         return pltpu.make_async_remote_copy(
-            src_ref=s_ref.at[phase, block(to), :],
-            dst_ref=d_ref.at[phase, block(slot), :],
-            send_sem=send_sem.at[sem_phase, chunk],
-            recv_sem=recv_sem.at[sem_phase, chunk],
+            src_ref=s_ref.at[(phase,) + src_at],
+            dst_ref=d_ref.at[(phase,) + dst_at],
+            send_sem=send_sem.at[trip, chunk],
+            recv_sem=recv_sem.at[trip, chunk],
             device_id={"gz": to},
             device_id_type=MESH,
         )
 
-    def start(sem_phase, chunk, offset, size, s_ref, d_ref):
+    def start(trip, chunk):
+        first, count, offset, size = chunks[trip][chunk]
+
+        def block(g):
+            return pl.ds(first, count), pl.ds(pl.multiple_of(offset + 32 * g, 8), size)
+
         for to in peers:
-            exchange_copy(sem_phase, chunk, offset, size, s_ref, d_ref, to, me).start()
-        phase = sem_phase // 2
-        own = pl.ds(pl.multiple_of(offset + 32 * me, 8), size)
-        d_ref[phase, own, :] = s_ref[phase, own, :]
-
-    def wait(sem_phase, chunk, offset, size, s_ref, d_ref, receive=True):
-        phase = sem_phase // 2
-        rows = pl.ds(0, (GZ - 1) * size)
-        copy = pltpu.make_async_remote_copy(
-            src_ref=s_ref.at[phase, rows, :],
-            dst_ref=d_ref.at[phase, rows, :],
-            send_sem=send_sem.at[sem_phase, chunk],
-            recv_sem=recv_sem.at[sem_phase, chunk],
-            device_id={"gz": peers[0]},
-            device_id_type=MESH,
-        )
+            exchange_copy(trip, chunk, block(to), block(me), to).start()
+        s_ref, d_ref = buffers[trip % 2]
+        for half in range(first, first + count):
+            own = (trip // 2, half, pl.ds(pl.multiple_of(offset + 32 * me, 8), size))
+            d_ref[own] = s_ref[own]
+
+    def wait(trip, chunk, receive=True):
+        first, count, offset, size = chunks[trip][chunk]
+        at = (pl.ds(0, count), pl.ds(0, (GZ - 1) * size))
+        copy = exchange_copy(trip, chunk, at, at, peers[0])
         if receive:
             copy.wait_recv()
         else:
             copy.wait_send()
-
-    back_chunks = ((0, 16), (16, 8), (24, 8), (1024, 32))
 
     def forward_second(field, phase, h, ph):
         x = jnp.concatenate(
@@ -247,7 +249,7 @@
         y = left_dft(aq[pl.ds(h * 256, 256), :], x)
         for g in range(GZ):
             for j in range(2):
-                y_buf[phase, pl.ds(h * 1024 + g * 32 + (2 * ph + j) * 8, 8), :] = y[
+                y_buf[phase, h, pl.ds(g * 32 + (2 * ph + j) * 8, 8), :] = y[
                     8 * g : 8 * g + 8, j * 128 : j * 128 + 128
                 ]
 
@@ -256,21 +258,20 @@
         def _(kk):
             h = kk // 2
 
-            @pl.when(lax.rem(kk, 2) == 0)
-            def _():
-                if phase == 0:
-                    wait(0, h, h * 1024, 32, y_buf, r_buf)
-                else:
-                    for ph in range(2):
-                        wait(2, 2 * ph + h, h * 1024 + ph * 16, 16, y_buf, r_buf)
+            for h_now, needed in (((0, (0,)), (1, (1,))), ((0, (0, 1)), (1, (2,))))[phase]:
+
+                @pl.when(kk == 2 * h_now)
+                def _():
+                    for chunk in needed:
+                        wait(2 * phase, chunk)
 
             cols = []
             for i in range(2):
                 rows = []
                 for c in range(2):
                     for p in range(4):
-                        first = h * 1024 + p * 8 + c * 4 + 2 * lax.rem(kk, 2) + i
-                        x = r_buf[phase, pl.ds(first, GZ, stride=32), :]
+                        first = p * 8 + c * 4 + 2 * lax.rem(kk, 2) + i
+                        x = r_buf[phase, h, pl.ds(first, GZ, stride=32), :]
                         if ratio is not None:
                             x = x + ratio * placed_freq[
                                 2 * kk + i, c * NC + p * GZ : c * NC + (p + 1) * GZ, :
@@ -296,19 +297,19 @@
             )
             for ph in range(2):
                 for g in range(GZ):
-                    at = pl.multiple_of(ph * 1024 + g * 32 + kk * 8, 8)
-                    u_buf[phase, pl.ds(at, 8), :] = halves_of_u[ph][8 * g : 8 * g + 8]
-
-            for at_kk, chunks in ((1, (0,)), (2, (1,)), (3, (2, 3))):
+                    at = pl.multiple_of(g * 32 + kk * 8, 8)
+                    u_buf[phase, ph, pl.ds(at, 8), :] = halves_of_u[ph][8 * g : 8 * g + 8]
+
+            for at_kk, done in (((1, (0,)), (2, (1,)), (3, (2, 3))), ((1, (0,)), (3, (1, 2))))[phase]:
 
                 @pl.when(kk == at_kk)
                 def _():
-                    for chunk in chunks:
-                        start(2 * phase + 1, chunk, *back_chunks[chunk], u_buf, b_buf)
+                    for chunk in done:
+                        start(2 * phase + 1, chunk)
 
     def wait_back(phase, ph):
-        for chunk in ((0, 1, 2), (3,))[ph]:
-            wait(2 * phase + 1, chunk, *back_chunks[chunk], u_buf, b_buf)
+        for chunk in (((0, 1, 2), (3,)), ((0, 1), (2,)))[phase][ph]:
+            wait(2 * phase + 1, chunk)
 
     def inverse_second(phase, ph):
         cols = []
@@ -317,8 +318,8 @@
             for c in range(2):
                 for kk in range(4):
                     for i in range(2):
-                        first = ph * 1024 + kk * 8 + i * 4 + c * 2 + p2
-                        rows.append(b_buf[phase, pl.ds(first, GZ, stride=32), :])
+                        first = kk * 8 + i * 4 + c * 2 + p2
+                        rows.append(b_buf[phase, ph, pl.ds(first, GZ, stride=32), :])
             cols.append(jnp.concatenate(rows, axis=0))
         return left_dft(aiq[...], jnp.concatenate(cols, axis=1))
 
@@ -328,7 +329,7 @@
             forward_second(src, 0, h, ph)
         if h == 0:
             pl.semaphore_wait(barrier, GZ - 1 + TX - 1)
-        start(0, h, h * 1024, 32, y_buf, r_buf)
+        start(0, h)
 
     def extra_copy(to, src_ref, dst_ref):
         return pltpu.make_async_remote_copy(
@@ -547,9 +548,13 @@
 
         return lax.fori_loop(0, 8, step, acc)
 
-    def drive_start(ph, h):
-        forward_second(drive, 1, h, ph)
-        start(2, 2 * ph + h, h * 1024 + ph * 16, 16, y_buf, r_buf)
+    def drive_start(ph):
+        for h in range(2):
+            forward_second(drive, 1, h, ph)
+            if ph == 1:
+                start(2, 1 + h)
+        if ph == 0:
+            start(2, 0)
 
     def misfit_copy(to, src_ref, dst_ref):
         return pltpu.make_async_remote_copy(
@@ -598,10 +603,9 @@
             both = found[c * NC : (c + 1) * NC] + found[(2 + c) * NC : (3 + c) * NC]
             sampled = jnp.sum(jnp.where(on_lane, both, 0.0), axis=0, keepdims=True)
             misfit.append(jnp.where(inside, meas[c : c + 1, :] - sampled, 0.0))
-        rest = jnp.zeros((6, 128), F32)
         for i in range(8):
             at = slice(i * 128, (i + 1) * 128)
-            mf[i] = jnp.concatenate([misfit[0][:, at], misfit[1][:, at], rest], axis=0)
+            mf[i] = jnp.concatenate([misfit[0][:, at], misfit[1][:, at]], axis=0)
         mf_in[me] = mf[me // 4]
 
         for to in peers:
@@ -652,20 +656,20 @@
             device_id_type=MESH,
         )
 
-    obj_most = obj_all.at[pl.ds(0, 8 * (GZ - 1)), :]
+    obj_most = obj_all.at[pl.ds(0, GZ - 1)]
     obj_wait = obj_copy(peers[0], obj_most, obj_most)
 
     def object_start(acc):
-        own = acc[0:8] + acc[8:16] + acc[16:24] + acc[24:32]
+        own = jnp.sum(acc, axis=0, keepdims=True)
         obj[...] = own
-        mine = pl.ds(pl.multiple_of(8 * me, 8), 8)
-        obj_all[mine, :] = own
+        obj_all[me] = own
         for to in peers:
-            obj_copy(to, obj, obj_all.at[mine, :]).start()
+            obj_copy(to, obj, obj_all.at[me]).start()
 
     def object_ratio():
         obj_wait.wait_recv()
-        object_norm = jnp.sum(obj_all[...], keepdims=True)
+        rows = jnp.concatenate([obj_all[g] for g in range(GZ)], axis=0)
+        object_norm = jnp.sum(rows, keepdims=True)
         data_norm = jnp.zeros((1, 1), F32)
         for j in range(TX):
             data_norm = data_norm + extra_all[8 * j : 8 * j + 1, 2:3]
@@ -675,20 +679,18 @@
     found_first[...] = found_at(0)
     ring_start(0)
     contrast_start(0)
+    fields(1)
     contrast_forward(0)
-    fields(1)
+    ring_start(1)
     misfit_start()
     acc = residual(0, jnp.zeros((32, 128), F32))
-    drive_start(0, 0)
-    ring_start(1)
-    drive_start(0, 1)
+    drive_start(0)
     contrast_start(1)
     misfit_forward()
     contrast_forward(1)
     acc = residual(1, acc)
     object_start(acc)
-    drive_start(1, 0)
-    drive_start(1, 1)
+    drive_start(1)
     placed_spectrum()
     chi_store = pltpu.make_async_copy(chi, chi_hbm, store_sem.at[2])
     chi_store.start()
@@ -708,13 +710,9 @@
         )
         stores[-1].start()
 
-    for h in range(2):
-        wait(0, h, h * 1024, 32, y_buf, r_buf, False)
-        for ph in range(2):
-            wait(2, 2 * ph + h, h * 1024 + ph * 16, 16, y_buf, r_buf, False)
-    for phase in range(2):
-        for chunk in range(4):
-            wait(2 * phase + 1, chunk, *back_chunks[chunk], u_buf, b_buf, False)
+    for trip in range(4):
+        for chunk in range(len(chunks[trip])):
+            wait(trip, chunk, False)
 
     chi_store.wait()
     for store in stores:
@@ -758,10 +756,10 @@
             buf(2, ROWS, 128),
             buf(2, 4096, 128),
             buf(2, 8, NP, NP),
-            buf(2, 2048, 128),
-            buf(2, 2048, 128),
-            buf(2, 2048, 128),
-            buf(2, 2048, 128),
+            buf(2, 2, 1024, 128),
+            buf(2, 2, 1024, 128),
+            buf(2, 2, 1024, 128),
+            buf(2, 2, 1024, 128),
             buf(2, ROWS, 128),
             buf(ROWS, 128),
             buf(2, ROWS, 128),
@@ -777,12 +775,12 @@
             buf(2, ROWS, 128),
             buf(8, 128),
             buf(64, 128),
-            buf(8, 128),
-            buf(256, 128),
-            buf(8, 8, 128),
-            buf(GZ, 8, 128),
-            buf(8, 128),
-            buf(8, 8, 128),
+            buf(1, 128),
+            buf(GZ, 1, 128),
+            buf(8, 2, 128),
+            buf(GZ, 2, 128),
+            buf(2, 128),
+            buf(8, 2, 128),
             buf(8, 2 * NC, 128),
             buf(512, NREC),
             dma((7,)),

time: 128 us -> 125 us (0.977)
  Pallas kernels: 123 us -> 121 us
    pallas_call x1, Pallas kernels: 123 us -> 121 us  [shards(): pl.pallas_call(kernel, out_shape=(field, field), in_specs=[hbm] * 5 + [pl...]
where the time goes in v5:
time: 125 us
  Pallas kernels  121 us (97%)
  local copies, waits for them, and re-layouts  3.74 us (3%)
    pallas_call x1, Pallas kernels, shards(): pl.pallas_call(kernel, out_shape=(field, field), in_specs=[hbm] * 5 + [pl...  121 us
    unnamed x2, local copies, waits for them, and re-layouts  3.74 us

profile of v5, /device:TPU:1, one launch (start us, length us, event | category | flops | bytes accessed | tf_op | source)
XLA Modules:
  0.0 125.0 jit_solution(6127410468299442733)
XLA Ops:
  0.6 120.6 %shard_map.86 = (f32[2,512,128]{2,1,0:T(8,128)}, f32[2,512,128]{2,1,0:T(8,128)}) custom-call(f32[2,512,128]{2,1,0:T(8,128)} %bitcast.9, f32[2,512,128]{2,1,0:T(8,128)} %bitcast.10, f32[4096,256]{1,0:T(8,128)} %bitcast.6, f32[2,1024]{1,0:T(2,128)} %bitcast.11, s32[1,1024]{1,0:T(1,128)} %cell_hbm.1, s32[1,2]{1,0:T(1,128)} %pos.1, ...), custom_call_target="tpu_custom_call" | custom-call | tf_op jit(solution)/shard_map/pallas_call | solution.py:740
  121.3 1.9 %copy.11 = f32[1,2,4,128,128]{4,3,2,1,0:T(8,128)} copy(f32[1,2,4,128,128]{4,3,2,1,0:T(8,128)} %bitcast.8) | data formatting | bytes 1048576
  123.2 1.9 %copy.12 = f32[2,4,128,128]{3,2,1,0:T(8,128)} copy(f32[2,4,128,128]{3,2,1,0:T(8,128)} %bitcast.7) | data formatting | bytes 1048576

commit v6 on v5

--- a/solution.py
+++ b/solution.py
@@ -198,7 +198,7 @@
         ((0, 1, 0, 32), (1, 1, 0, 32)),
         ((0, 1, 0, 16), (0, 1, 16, 8), (0, 1, 24, 8), (1, 1, 0, 32)),
         ((0, 2, 0, 16), (0, 1, 16, 16), (1, 1, 16, 16)),
-        ((0, 2, 0, 16), (0, 1, 16, 16), (1, 1, 16, 16)),
+        ((0, 2, 0, 8), (0, 2, 8, 8), (0, 1, 16, 16), (1, 1, 16, 16)),
     )
     buffers = ((y_buf, r_buf), (u_buf, b_buf))
 
@@ -300,7 +300,7 @@
                     at = pl.multiple_of(g * 32 + kk * 8, 8)
                     u_buf[phase, ph, pl.ds(at, 8), :] = halves_of_u[ph][8 * g : 8 * g + 8]
 
-            for at_kk, done in (((1, (0,)), (2, (1,)), (3, (2, 3))), ((1, (0,)), (3, (1, 2))))[phase]:
+            for at_kk, done in (((1, (0,)), (2, (1,)), (3, (2, 3))), ((0, (0,)), (1, (1,)), (3, (2, 3))))[phase]:
 
                 @pl.when(kk == at_kk)
                 def _():
@@ -308,7 +308,7 @@
                         start(2 * phase + 1, chunk)
 
     def wait_back(phase, ph):
-        for chunk in (((0, 1, 2), (3,)), ((0, 1), (2,)))[phase][ph]:
+        for chunk in ((0, 1, 2), (3,))[ph]:
             wait(2 * phase + 1, chunk)
 
     def inverse_second(phase, ph):
@@ -680,9 +680,9 @@
     ring_start(0)
     contrast_start(0)
     fields(1)
+    misfit_start()
+    ring_start(1)
     contrast_forward(0)
-    ring_start(1)
-    misfit_start()
     acc = residual(0, jnp.zeros((32, 128), F32))
     drive_start(0)
     contrast_start(1)
@@ -726,6 +726,22 @@
         chi_wait(ph).wait_send()
         core_copy(ph).wait_send()
         chi_send(ph, core).wait_send()
+
+
+def deliver_kernel(new_in, chi_in, new_out, chi_out):
+    new_out[...] = new_in[...]
+    chi_out[...] = chi_in[...]
+
+
+def deliver(new, chi):
+    block = pl.BlockSpec(memory_space=pltpu.VMEM)
+    shape = jax.ShapeDtypeStruct((2, ROWS, 128), F32)
+    return pl.pallas_call(
+        deliver_kernel,
+        out_shape=(shape, shape),
+        in_specs=(block, block),
+        out_specs=(block, block),
+    )(new, chi)
 
 
 def shards(sources, contrast, spectrum, measured, receivers, positions):
@@ -803,6 +819,7 @@
         positions,
         table,
     )
+    new, chi = deliver(new, chi)
     return new.reshape(sources.shape), chi.reshape(contrast.shape)
 
 

time: 125 us -> 121 us (0.968)
  local copies, waits for them, and re-layouts: 3.74 us -> 0 us
    unnamed x2 -> x0, local copies, waits for them, and re-layouts: 3.74 us -> none
    pallas_call x1, Pallas kernels: 121 us -> 118 us  [shards(): pl.pallas_call(kernel, out_shape=(field, field), in_specs=[hbm] * 5 + [pl...]
    pallas_call x0 -> x1, Pallas kernels: none -> 2.2 us  [deliver(): pl.pallas_call(deliver_kernel, out_shape=(shape, shape), in_specs=(block,...]
where the time goes in v6:
time: 121 us
  Pallas kernels  120 us (99%)
    pallas_call x1, Pallas kernels, shards(): pl.pallas_call(kernel, out_shape=(field, field), in_specs=[hbm] * 5 + [pl...  118 us

profile of v6, /device:TPU:1, one launch (start us, length us, event | category | flops | bytes accessed | tf_op | source)
XLA Modules:
  0.0 120.9 jit_solution(10818206387029162176)
XLA Ops:
  0.6 118.1 %shard_map.86 = (f32[2,512,128]{2,1,0:T(8,128)}, f32[2,512,128]{2,1,0:T(8,128)}) custom-call(f32[2,512,128]{2,1,0:T(8,128)} %bitcast.7, f32[2,512,128]{2,1,0:T(8,128)} %bitcast.8, f32[4096,256]{1,0:T(8,128)} %bitcast.6, f32[2,1024]{1,0:T(2,128)} %bitcast.9, s32[1,1024]{1,0:T(1,128)} %cell_hbm.1, s32[1,2]{1,0:T(1,128)} %pos.1, ...), custom_call_target="tpu_custom_call" | custom-call | tf_op jit(solution)/shard_map/pallas_call | solution.py:756
  118.7 2.2 %shard_map.87 = (f32[2,512,128]{2,1,0:T(8,128)}, f32[2,512,128]{2,1,0:T(8,128)}) custom-call(f32[2,512,128]{2,1,0:T(8,128)} %get-tuple-element.6.new_in, f32[2,512,128]{2,1,0:T(8,128)} %get-tuple-element.7.chi_in), custom_call_target="tpu_custom_call" | custom-call | tf_op jit(solution)/shard_map/pallas_call | solution.py:739

commit v7 on v6

--- a/solution.py
+++ b/solution.py
@@ -132,12 +132,12 @@
 
 
 def kernel(
-    src_hbm, contrast_hbm, spec_hbm, meas_hbm, cell_hbm, pos,
+    src_hbm, contrast_hbm, spec_hbm, meas_hbm, cell_hbm, pos_hbm,
     aq_hbm,
     new_hbm, chi_hbm,
-    src, contrast, meas, cell, aq, ap, br, bir, aip, aiq, out_src,
+    src, contrast, meas, cell, pos, aq, ap, br, bir, aip, aiq, out_src,
     spec_raw, spec, y_buf, r_buf, u_buf, b_buf, inc, amp_sum, scat, res, drive,
-    hot, hot_plane, part, half_in, half_sum, ring_in, chi_own, chi, extra, extra_all,
+    hot, hot_plane, part, ring_in, chi_own, chi, extra, extra_all,
     obj, obj_all, mf, mf_in, mf_own, mf_all, placed_freq, found_first,
     load_sem, store_sem, send_sem, recv_sem, tx_send, tx_recv, ex_send, ex_recv,
     ob_send, ob_recv, ma_send, ma_recv, mb_send, mb_recv,
@@ -164,6 +164,7 @@
             ("src", src_hbm, src),
             ("meas", meas_hbm, meas),
             ("cell", cell_hbm, cell),
+            ("pos", pos_hbm, pos),
             ("spec0", spec_hbm.at[:, pl.ds(0, 128)], spec_raw.at[0]),
             ("spec1", spec_hbm.at[:, pl.ds(128, 128)], spec_raw.at[1]),
             ("contrast", contrast_hbm, contrast),
@@ -184,12 +185,12 @@
 
     for load in loads.values():
         load.start()
-    loaded("meas")
+    loaded("meas", "pos")
 
     lane = lax.broadcasted_iota(jnp.int32, (8, 128), 1)
     share = jnp.sum(meas[...] * meas[...], keepdims=True)
-    row = jnp.where(lane == 0, pos[0, 0].astype(F32), 0.0)
-    row = row + jnp.where(lane == 1, pos[0, 1].astype(F32), 0.0)
+    row = jnp.where(lane == 0, pos[0:1, 0:1].astype(F32), 0.0)
+    row = row + jnp.where(lane == 1, pos[0:1, 1:2].astype(F32), 0.0)
     row = row + jnp.where(lane == 2, share, 0.0)
     extra[...] = row
     extra_all[pl.ds(pl.multiple_of(8 * tx, 8), 8), :] = row
@@ -356,8 +357,8 @@
     @pl.loop(0, 16)
     def _(n):
         a, b, c = geometry(n, 32)
-        b = b - pos[0, 0]
-        c = c - pos[0, 1]
+        b = b - pos[0:1, 0:1]
+        c = c - pos[0:1, 1:2]
         radius = jnp.sqrt((a * a + b * b + c * c).astype(F32))
         amplitude = reach_cells / (reach_cells + radius)
         sine, cosine = sin_cos_twelfth(radius)
@@ -434,22 +435,19 @@
     def plane_rows(p):
         return pl.ds(pl.multiple_of(p * NC, NC), NC)
 
-    def core_copy(ph):
-        return to_partner(part.at[:, plane_rows(2 * ph + 1 - core), :], half_in.at[ph], 4 * ph)
-
     def ring_copy(ph, to, src_ref, dst_ref):
         return pltpu.make_async_remote_copy(
             src_ref=src_ref,
             dst_ref=dst_ref,
             send_sem=tx_send.at[4 * ph + 1],
             recv_sem=tx_recv.at[4 * ph + 1],
-            device_id={"tx": 2 * to + core},
+            device_id={"tx": to},
             device_id_type=MESH,
         )
 
     def ring_wait(ph):
-        three = ring_in.at[ph, pl.ds(0, 3)]
-        return ring_copy(ph, x_peers[0], three, three)
+        seven = ring_in.at[ph, pl.ds(0, TX - 1)]
+        return ring_copy(ph, tx_peers[0], seven, seven)
 
     def own_rows(ph, x):
         return pl.ds(pl.multiple_of((2 * ph + core) * NC + x * 32, 32), 32)
@@ -492,31 +490,23 @@
             part[1, at, :] = si * tr - sr * ti
             part[2, at, :] = tr * tr + ti * ti
 
-        core_copy(ph).start()
-
-    def ring_start(ph):
-        core_copy(ph).wait_recv()
-        for q in range(3):
-            half_sum[ph, q] = part[q, plane_rows(2 * ph + core), :] + half_in[ph, q]
-
-        for to in x_peers:
-            ring_copy(
-                ph,
-                to,
-                half_sum.at[ph, :, pl.ds(pl.multiple_of(to * 32, 32), 32), :],
-                ring_in.at[ph, my_x],
-            ).start()
-
-        ring_in[ph, my_x] = half_sum[ph, :, pl.ds(pl.multiple_of(my_x * 32, 32), 32), :]
+        def share(t):
+            first = (2 * ph + lax.rem(t, 2)) * NC + (t // 2) * 32
+            return pl.ds(pl.multiple_of(first, 32), 32)
+
+        for to in tx_peers:
+            ring_copy(ph, to, part.at[:, share(to), :], ring_in.at[ph, tx]).start()
+        ring_in[ph, tx] = part[:, share(tx), :]
 
     def contrast_start(ph):
         ring_wait(ph).wait_recv()
 
         sums = []
         for q in range(3):
-            sums.append(
-                ring_in[ph, 0, q] + ring_in[ph, 1, q] + ring_in[ph, 2, q] + ring_in[ph, 3, q]
-            )
+            total = ring_in[ph, 0, q]
+            for t in range(1, TX):
+                total = total + ring_in[ph, t, q]
+            sums.append(total)
         below = sums[2] + tikhonov
         rows = own_rows(ph, my_x)
         for c in range(2):
@@ -677,11 +667,9 @@
 
     fields(0)
     found_first[...] = found_at(0)
-    ring_start(0)
     contrast_start(0)
     fields(1)
     misfit_start()
-    ring_start(1)
     contrast_forward(0)
     acc = residual(0, jnp.zeros((32, 128), F32))
     drive_start(0)
@@ -724,7 +712,6 @@
     for ph in range(2):
         ring_wait(ph).wait_send()
         chi_wait(ph).wait_send()
-        core_copy(ph).wait_send()
         chi_send(ph, core).wait_send()
 
 
@@ -756,13 +743,14 @@
     new, chi = pl.pallas_call(
         kernel,
         out_shape=(field, field),
-        in_specs=[hbm] * 5 + [pl.BlockSpec(memory_space=pltpu.SMEM), hbm],
+        in_specs=[hbm] * 7,
         out_specs=(hbm, hbm),
         scratch_shapes=[
             buf(2, ROWS, 128),
             buf(2, ROWS, 128),
             buf(2, NREC),
             pltpu.VMEM((1, NREC), jnp.int32),
+            pltpu.VMEM((1, 2), jnp.int32),
             pltpu.VMEM((512, 512), BF16),
             pltpu.VMEM((512, 512), BF16),
             pltpu.VMEM((512, 512), BF16),
@@ -784,9 +772,7 @@
             pltpu.VMEM((ROWS, NREC), BF16),
             pltpu.VMEM((NC, NREC), BF16),
             buf(3, ROWS, 128),
-            buf(2, 3, NC, 128),
-            buf(2, 3, NC, 128),
-            buf(2, 4, 3, 32, 128),
+            buf(2, TX, 3, 32, 128),
             buf(2, 2, 32, 128),
             buf(2, ROWS, 128),
             buf(8, 128),
@@ -799,7 +785,7 @@
             buf(8, 2, 128),
             buf(8, 2 * NC, 128),
             buf(512, NREC),
-            dma((7,)),
+            dma((8,)),
             dma((3,)),
             dma((4, 4)),
             dma((4, 4)),

time: 121 us -> 119 us (0.983)
  Pallas kernels: 120 us -> 118 us
    pallas_call x1, Pallas kernels: 118 us -> 116 us  [shards(): pl.pallas_call(kernel, out_shape=(field, field), in_specs=[hbm] * 7, out_...]
where the time goes in v7:
time: 119 us
  Pallas kernels  118 us (99%)
    pallas_call x1, Pallas kernels, shards(): pl.pallas_call(kernel, out_shape=(field, field), in_specs=[hbm] * 7, out_...  116 us

profile of v7, /device:TPU:1, one launch (start us, length us, event | category | flops | bytes accessed | tf_op | source)
XLA Modules:
  0.0 118.9 jit_solution(9261873995315702035)
XLA Ops:
  0.6 116.0 %shard_map.86 = (f32[2,512,128]{2,1,0:T(8,128)}, f32[2,512,128]{2,1,0:T(8,128)}) custom-call(f32[2,512,128]{2,1,0:T(8,128)} %bitcast.7, f32[2,512,128]{2,1,0:T(8,128)} %bitcast.8, f32[4096,256]{1,0:T(8,128)} %bitcast.6, f32[2,1024]{1,0:T(2,128)} %bitcast.9, s32[1,1024]{1,0:T(1,128)} %cell_hbm.1, s32[1,2]{1,0:T(1,128)} %pos_hbm.1, ...), custom_call_target="tpu_custom_call" | custom-call | tf_op jit(solution)/shard_map/pallas_call | solution.py:743
  116.7 2.2 %shard_map.87 = (f32[2,512,128]{2,1,0:T(8,128)}, f32[2,512,128]{2,1,0:T(8,128)}) custom-call(f32[2,512,128]{2,1,0:T(8,128)} %get-tuple-element.6.new_in, f32[2,512,128]{2,1,0:T(8,128)} %get-tuple-element.7.chi_in), custom_call_target="tpu_custom_call" | custom-call | tf_op jit(solution)/shard_map/pallas_call | solution.py:726
